TPU v7x, 32 devices: a whole 2x2x4 slice. The times are simulated.
32 devices in a mesh: row: 8 (over y, x, core), col: 4 (over z).
Axes of the slice: x: 2, y: 2, z: 4, core: 2. Of those that a mesh axis runs over, the one named last changes fastest.
Arguments:
- points: bfloat16 [16, 16384], P(None, ('row', 'col')), may hold values from -6 to 6
- spread: bfloat16 [16384], P(('row', 'col')), may hold values from 2 to 12
- vectors: bfloat16 [8, 16384], P(None, ('row', 'col')), may hold values from -6 to 6
Outputs:
- basis: float32 [8, 16384], P(None, ('row', 'col'))
All inputs are finite; a program needn't handle non-finite values.
Results may differ from a plain program's by a relative error of at most 0.012.
Values may be sent and summed in bfloat16 or wider, within the bound.
No kernel may reach another device: no remote copies, remote signals or barrier semaphores. Data moves between devices by JAX's collectives and lax.ppermute only.
A program may use at most 64 MiB of HBM per device.

v0:
```python
import functools
import math

import jax
import jax.numpy as jnp
from jax import lax
from jax.experimental import pallas as pl
from jax.experimental.pallas import tpu as pltpu
from jax.sharding import PartitionSpec as P


VMEM = pl.BlockSpec(memory_space=pltpu.VMEM)
F32 = jnp.float32
BF16 = jnp.bfloat16
AUX = 8
ONE, SCALE = 3, 4


def call(kernel, out_shape, *args, scratch=(), out_vmem=True, in_hbm=False, flops=10**6, moved=10**5, exps=0, limit=16 * 2**20):
    return pl.pallas_call(
        kernel,
        out_shape=jax.tree.map(lambda s: pltpu.VMEM(s.shape, s.dtype), out_shape) if out_vmem else out_shape,
        in_specs=[VMEM] * len(args),
        out_specs=jax.tree.map(lambda _: VMEM, out_shape),
        scratch_shapes=scratch,
        cost_estimate=pl.CostEstimate(flops=flops, bytes_accessed=moved, transcendentals=exps),
        compiler_params=pltpu.CompilerParams(vmem_limit_bytes=limit),
    )(*[pltpu.with_memory_space_constraint(x, pltpu.HBM if in_hbm else pltpu.VMEM) for x in args])


def three_parts(x):
    hi = x.astype(BF16).astype(F32)
    rest = x - hi
    mid = rest.astype(BF16).astype(F32)
    return hi, mid, rest - mid


def span_of(dims, kvec, local):
    return (dims + kvec) // AUX * local + 128 * (-(-local // (128 * AUX)))


def pack_kernel(points_ref, spread_ref, vectors_ref, out_ref):
    local = points_ref.shape[1]
    at = 0
    for ref in (points_ref, vectors_ref):
        for top in range(0, ref.shape[0], AUX):
            out_ref[:, at : at + local] = ref[top : top + AUX, :]
            at += local
    spread = spread_ref[...].reshape(1, local).astype(F32)
    for column in range(0, local, 128 * AUX):
        pieces = [spread[:, i : i + 128] for i in range(column, min(local, column + 128 * AUX), 128)]
        out_ref[:, at : at + 128] = place_rows(pieces, 128).astype(BF16)
        at += 128


def place_rows(entries, width):
    row = lax.broadcasted_iota(jnp.int32, (AUX, width), 0)
    out = jnp.ones((AUX, width), F32)
    for place, entry in enumerate(entries):
        out = jnp.where(row == place, entry, out)
    return out


def expand(ref, at, dims, kvec, local):
    groups = [
        ref[:, pl.ds(at + i * local, local)].astype(F32) for i in range((dims + kvec) // AUX)
    ]
    points = jnp.concatenate(groups[: dims // AUX], axis=0)
    base = at + len(groups) * local
    spread = []
    for i in range(local // 128):
        tile = ref[:, pl.ds(base + i // AUX * 128, 128)].astype(F32)
        spread.append(tile[i % AUX : i % AUX + 1])
    norm = jnp.sum(points * points, axis=0, keepdims=True)
    aux = place_rows((*three_parts(norm), jnp.ones_like(norm), jnp.concatenate(spread, axis=1)), local)
    return jnp.concatenate([points, aux, *groups[dims // AUX :]], axis=0)


def left_factor(rows, dims):
    at = lambda i: rows[dims + i : dims + i + 1]
    rate = F32(math.log2(math.e)) / at(SCALE)
    norm = at(0) + at(1) + at(2)
    row = lax.broadcasted_iota(jnp.int32, (AUX, rows.shape[1]), 0)
    aux = jnp.where(row < ONE, -rate, jnp.where(row == ONE, -norm * rate, F32(0)))
    factor = jnp.concatenate(
        [2 * rate * rows[:dims], aux, jnp.zeros((rows.shape[0] - dims - AUX, rows.shape[1]), F32)], axis=0
    )
    parts = three_parts(factor)
    return jnp.concatenate([*parts, jnp.zeros_like(factor)], axis=0)


def accumulate(left_ref, block_ref, acc_ref, sizes, tall):
    dims, _, _ = sizes
    rows, span = left_ref.shape[0], span_of(*sizes)
    count = block_ref.shape[1] // span

    def step(c, carry):
        full = expand(block_ref, pl.multiple_of(c * span, 128), *sizes)
        rate = 1.0 / full[dims + SCALE : dims + SCALE + 1]
        block = full.astype(BF16)
        right = jnp.concatenate([block] * 4, axis=0)
        for m in range(0, rows, tall):
            exponent = lax.dot_general(
                left_ref[m : m + tall, :], right, (((1,), (0,)), ((), ())), preferred_element_type=F32
            )
            affinity = jnp.exp2(exponent * rate).astype(BF16)
            acc_ref[:, m : m + tall] += lax.dot_general(
                block, affinity, (((1,), (1,)), ((), ())), preferred_element_type=F32
            )
        return carry

    if count == 1:
        step(0, 0)
    else:
        lax.fori_loop(0, count, step, 0, unroll=min(count, 3))


def own_kernel(sizes, tall, own_ref, mate_ref, left_ref, acc_ref):
    dims, _, local = sizes
    left_ref[:local, :] = left_factor(expand(own_ref, 0, *sizes), dims).T.astype(BF16)
    left_ref[local:, :] = left_factor(expand(mate_ref, 0, *sizes), dims).T.astype(BF16)
    acc_ref[...] = jnp.zeros_like(acc_ref)

    @pl.when(lax.axis_index("row") % 2 == 1)
    def _():
        accumulate(left_ref, own_ref, acc_ref, sizes, tall)
        accumulate(left_ref, mate_ref, acc_ref, sizes, tall)


def add_kernel(sizes, tall, left_ref, part_ref, *refs):
    *block_refs, acc_ref = refs
    acc_ref[...] = part_ref[...]
    for block_ref in block_refs:
        accumulate(left_ref, block_ref, acc_ref, sizes, tall)


def last_kernel(sizes, tall, left_ref, part_ref, *refs):
    *block_refs, out_ref, acc_ref = refs
    add_kernel(sizes, tall, left_ref, part_ref, *block_refs, acc_ref)
    out_ref[...] = acc_ref[sizes[0] :, :]


def join_kernel(*refs):
    *block_refs, out_ref = refs
    at = 0
    for block_ref in block_refs:
        out_ref[:, at : at + block_ref.shape[1]] = block_ref[...]
        at += block_ref.shape[1]


def sum_kernel(*refs):
    *part_refs, out_ref = refs
    out_ref[...] = functools.reduce(lambda a, b: a + b, [ref[...] for ref in part_refs])


def update_kernel(mine_ref, other_ref, update_ref, gram_ref):
    local = update_ref.shape[1]
    own = mine_ref[:, :local] + other_ref[:, local:]
    mate = mine_ref[:, local:] + other_ref[:, :local]
    own = own[AUX:] / own[ONE : ONE + 1]
    mate = mate[AUX:] / mate[ONE : ONE + 1]
    update_ref[...] = own
    kvec = own.shape[0]
    column = lax.broadcasted_iota(jnp.int32, gram_ref.shape, 1)
    gram = jnp.zeros(gram_ref.shape, F32)
    for k in range(kvec):
        with_k = jnp.sum(own * own[k : k + 1] + mate * mate[k : k + 1], axis=1, keepdims=True)
        gram = jnp.where(column == k, with_k, gram)
    gram_ref[...] = gram


def basis_kernel(root, update_ref, *refs):
    *gram_refs, out_ref = refs
    gram = functools.reduce(lambda a, b: a + b, [ref[...] for ref in gram_refs])
    rest = update_ref[...]
    kvec = rest.shape[0]
    row = lax.broadcasted_iota(jnp.int32, gram.shape, 0)
    column = lax.broadcasted_iota(jnp.int32, gram.shape, 1)
    for k in range(kvec - 1):
        factor = jnp.where(row[:, :1] > k, gram[:, k : k + 1] / gram[k : k + 1, k : k + 1], F32(0))
        rest = rest - factor * rest[k : k + 1]
        gram = gram - factor * gram[k : k + 1]
    pivot = jnp.sum(jnp.where(row == column, gram, F32(0)), axis=1, keepdims=True)
    out_ref[...] = rest * (root / jnp.sqrt(pivot))


def partners(count, step):
    if count & (count - 1) == 0:
        return [i ^ step for i in range(count)]
    return [(i + step) % count for i in range(count)]


def step(points, spread, vectors):
    n_row, n_col = lax.axis_size("row"), lax.axis_size("col")
    dims, local = points.shape
    kvec = vectors.shape[0]
    packed = dims + AUX + kvec
    sizes = (dims, kvec, local)
    span = span_of(*sizes)
    chips = n_row // 2

    def to_mate(x):
        return lax.ppermute(x, "row", [(i, i ^ 1) for i in range(n_row)])

    def along(x):
        return [lax.ppermute(x, "col", list(enumerate(partners(n_col, step)))) for step in range(1, n_col)]

    def across(x):
        return [
            lax.ppermute(
                x, "row", [(2 * i + core, 2 * j + core) for i, j in enumerate(partners(chips, step)) for core in (0, 1)]
            )
            for step in range(1, chips)
        ]

    shape = jax.ShapeDtypeStruct
    block = call(pack_kernel, shape((AUX, span), BF16), points, spread, vectors, in_hbm=True)
    mate = to_mate(block)
    column = along(block)
    beside = across(block)

    tall = math.gcd(2 * local, 1024)

    def size(blocks):
        pairs = 2 * local * blocks * local
        return dict(flops=2 * 2 * pairs * 160, exps=pairs, moved=10**6)

    left, part = call(
        functools.partial(own_kernel, sizes, tall),
        (shape((2 * local, 4 * packed), BF16), shape((packed, 2 * local), F32)),
        block, mate, **size(1),
    )
    column, left, part = lax.optimization_barrier((column, left, part))
    joined = call(join_kernel, shape((AUX, span * (n_col - 1)), BF16), *column)
    far = across(joined)
    near = [*column, *beside]
    part = call(
        functools.partial(add_kernel, sizes, tall),
        shape((packed, 2 * local), F32), left, part, *near, **size(len(near)),
    )
    for index, block in enumerate(far[::-1]):
        final = index == len(far) - 1
        part = call(
            functools.partial(last_kernel if final else add_kernel, sizes, tall),
            shape((packed - dims if final else packed, 2 * local), F32),
            left, part, block,
            scratch=[pltpu.VMEM((packed, 2 * local), F32)] * final,
            **size(n_col - 1),
        )
    update, gram = call(update_kernel, (shape((kvec, local), F32), shape((kvec, 128), F32)), part, to_mate(part))
    gram = call(sum_kernel, shape(gram.shape, F32), gram, *along(gram))
    root = math.sqrt(local * n_row * n_col)
    return call(
        functools.partial(basis_kernel, root), shape((kvec, local), F32), update, gram, *across(gram), out_vmem=False
    )


def solution(mesh):
    in_specs = (P(None, ("row", "col")), P(("row", "col")), P(None, ("row", "col")))
    out_specs = P(None, ("row", "col"))
    return jax.shard_map(step, mesh=mesh, in_specs=in_specs, out_specs=out_specs, check_vma=False)
```

profile of v0, /device:TPU:0, one launch (start us, length us, event | category | flops | bytes accessed | tf_op | source)
XLA Modules:
  0.0 42.4 jit_solution(13825767408396896514)
XLA Ops:
  0.0 0.7 %shard_map.37.own_ref = bf16[8,1664]{1,0:T(8,128)(2,1)S(1)} custom-call(bf16[16,512]{1,0:T(8,128)(2,1)} %points_ref.1, bf16[512]{0:T(512)(128)(2,1)} %spread_ref.1, bf16[8,512]{1,0:T(8,128)(2,1)} %vectors_ref.1), custom_call_target="tpu_custom_call" | custom-call | flops 1000000 | bytes 100000 | tf_op jit(solution)/shard_map/pallas_call | solution.py:20
  0.7 3.1 %collective-permute-start = (bf16[8,1664]{1,0:T(8,128)(2,1)S(1)}, bf16[8,1664]{1,0:T(8,128)(2,1)S(1)}, u32[]{:S(2)}, u32[]{:S(2)}) collective-permute-start(bf16[8,1664]{1,0:T(8,128)(2,1)S(1)} %shard_map.37.own_ref), channel_id=1, source_target_pairs={{0,1},{1,0},{2,3},{3,2},{4,5},{5,4},{6,7},{7,6},{8,9},{9,8},{10,11... | collective-permute-start | bytes 79880 | tf_op jit(solution)/shard_map/ppermute | solution.py:206
  3.9 2.6 %collective-permute-start.1 = (bf16[8,1664]{1,0:T(8,128)(2,1)S(1)}, bf16[8,1664]{1,0:T(8,128)(2,1)S(1)}, u32[]{:S(2)}, u32[]{:S(2)}) collective-permute-start(bf16[8,1664]{1,0:T(8,128)(2,1)S(1)} %shard_map.37.own_ref), channel_id=1, source_target_pairs={{0,2},{1,3},{2,0},{3,1},{4,6},{5,7},{6,4},{7,5},{8,10},{9,11},{10,... | collective-permute-start | bytes 79880 | tf_op jit(solution)/shard_map/ppermute | solution.py:206
  6.5 1.7 %collective-permute-start.4 = (bf16[8,1664]{1,0:T(8,128)(2,1)S(1)}, bf16[8,1664]{1,0:T(8,128)(2,1)S(1)}, u32[]{:S(2)}, u32[]{:S(2)}) collective-permute-start(bf16[8,1664]{1,0:T(8,128)(2,1)S(1)} %shard_map.37.own_ref), channel_id=1, source_target_pairs={{0,8},{4,12},{8,0},{12,4},{16,24},{20,28},{24,16},{28,20},{1,9},{5... | collective-permute-start | bytes 79880 | tf_op jit(solution)/shard_map/ppermute | solution.py:210
  8.2 1.5 %collective-permute-start.5 = (bf16[8,1664]{1,0:T(8,128)(2,1)S(1)}, bf16[8,1664]{1,0:T(8,128)(2,1)S(1)}, u32[]{:S(2)}, u32[]{:S(2)}) collective-permute-start(bf16[8,1664]{1,0:T(8,128)(2,1)S(1)} %shard_map.37.own_ref), channel_id=1, source_target_pairs={{0,16},{4,20},{8,24},{12,28},{16,0},{20,4},{24,8},{28,12},{1,17},{... | collective-permute-start | bytes 79880 | tf_op jit(solution)/shard_map/ppermute | solution.py:210
  9.7 0.3 collective-permute-start.6
  10.0 0.2 shard_map.38
  10.1 2.0 %collective-permute-done.2.refs_2_ = bf16[8,1664]{1,0:T(8,128)(2,1)S(1)} collective-permute-done((bf16[8,1664]{1,0:T(8,128)(2,1)S(1)}, bf16[8,1664]{1,0:T(8,128)(2,1)S(1)}, u32[]{:S(2)}, u32[]{:S(2)}) %collective-permute-start.2) | collective-permute-done | bytes 26656 | tf_op jit(solution)/shard_map/ppermute | solution.py:206
  12.1 2.5 %collective-permute-start.7 = (bf16[8,4992]{1,0:T(8,128)(2,1)S(1)}, bf16[8,4992]{1,0:T(8,128)(2,1)S(1)}, u32[]{:S(2)}, u32[]{:S(2)}) collective-permute-start(bf16[8,4992]{1,0:T(8,128)(2,1)S(1)} %shard_map.40), channel_id=1, source_target_pairs={{0,24},{4,28},{8,16},{12,20},{16,8},{20,12},{24,0},{28,4},{1,25},{... | collective-permute-start | bytes 239624 | tf_op jit(solution)/shard_map/ppermute | solution.py:210
  14.6 0.5 %collective-permute-start.8 = (bf16[8,4992]{1,0:T(8,128)(2,1)S(1)}, bf16[8,4992]{1,0:T(8,128)(2,1)S(1)}, u32[]{:S(2)}, u32[]{:S(2)}) collective-permute-start(bf16[8,4992]{1,0:T(8,128)(2,1)S(1)} %shard_map.40), channel_id=1, source_target_pairs={{0,16},{4,20},{8,24},{12,28},{16,0},{20,4},{24,8},{28,12},{1,17},{... | collective-permute-start | bytes 239624 | tf_op jit(solution)/shard_map/ppermute | solution.py:210
  15.1 0.5 %collective-permute-start.9 = (bf16[8,4992]{1,0:T(8,128)(2,1)S(1)}, bf16[8,4992]{1,0:T(8,128)(2,1)S(1)}, u32[]{:S(2)}, u32[]{:S(2)}) collective-permute-start(bf16[8,4992]{1,0:T(8,128)(2,1)S(1)} %shard_map.40), channel_id=1, source_target_pairs={{0,8},{4,12},{8,0},{12,4},{16,24},{20,28},{24,16},{28,20},{1,9},{5... | collective-permute-start | bytes 239624 | tf_op jit(solution)/shard_map/ppermute | solution.py:210
  15.7 3.4 %shard_map.39.part_ref = f32[32,1024]{1,0:T(8,128)S(1)} custom-call(bf16[1024,128]{1,0:T(8,128)(2,1)S(1)} %get-tuple-element.16.left_ref, f32[32,1024]{1,0:T(8,128)S(1)} %get-tuple-element.17.part_ref, bf16[8,1664]{1,0:T(8,128)(2,1)S(1)} %collective-permute-done.refs_0_, bf16[8,1664]{1,0:T(8,128)(2,1)S(1)} %collective-permute-done.1.refs_1_, ...), custom_call_target="tpu_custom_call" | custom-call | flops 2013265920 | bytes 1000000 | tf_op jit(solution)/shard_map/pallas_call | solution.py:20
  19.0 0.0 collective-permute-done.7.refs_0_
  19.1 1.7 %shard_map.41.part_ref = f32[32,1024]{1,0:T(8,128)S(1)} custom-call(bf16[1024,128]{1,0:T(8,128)(2,1)S(1)} %get-tuple-element.16.left_ref, f32[32,1024]{1,0:T(8,128)S(1)} %shard_map.39.part_ref, bf16[8,4992]{1,0:T(8,128)(2,1)S(1)} %collective-permute-done.7.refs_0_), custom_call_target="tpu_custom_call" | custom-call | flops 1006632960 | bytes 1000000 | tf_op jit(solution)/shard_map/pallas_call | solution.py:20
  20.8 1.7 %shard_map.42.part_ref = f32[32,1024]{1,0:T(8,128)S(1)} custom-call(bf16[1024,128]{1,0:T(8,128)(2,1)S(1)} %get-tuple-element.16.left_ref, f32[32,1024]{1,0:T(8,128)S(1)} %shard_map.41.part_ref, bf16[8,4992]{1,0:T(8,128)(2,1)S(1)} %collective-permute-done.8.refs_0_), custom_call_target="tpu_custom_call" | custom-call | flops 1006632960 | bytes 1000000 | tf_op jit(solution)/shard_map/pallas_call | solution.py:20
  22.6 0.0 collective-permute-done.9.refs_0_
  22.6 1.7 %shard_map.43.mine_ref = f32[16,1024]{1,0:T(8,128)S(1)} custom-call(bf16[1024,128]{1,0:T(8,128)(2,1)S(1)} %get-tuple-element.16.left_ref, f32[32,1024]{1,0:T(8,128)S(1)} %shard_map.42.part_ref, bf16[8,4992]{1,0:T(8,128)(2,1)S(1)} %collective-permute-done.9.refs_0_), custom_call_target="tpu_custom_call" | custom-call | flops 1006632960 | bytes 1000000 | tf_op jit(solution)/shard_map/pallas_call | solution.py:20
  24.3 0.1 collective-permute-start.10
  24.4 1.2 %collective-permute-done.10.other_ref = f32[16,1024]{1,0:T(8,128)S(1)} collective-permute-done((f32[16,1024]{1,0:T(8,128)S(1)}, f32[16,1024]{1,0:T(8,128)S(1)}, u32[]{:S(2)}, u32[]{:S(2)}) %collective-permute-start.10) | collective-permute-done | bytes 65568 | tf_op jit(solution)/shard_map/ppermute | solution.py:203
  25.6 0.1 shard_map.44
  25.7 0.0 collective-permute-start.11
  25.8 3.1 %collective-permute-start.12 = (f32[8,128]{1,0:T(8,128)S(1)}, f32[8,128]{1,0:T(8,128)S(1)}, u32[]{:S(2)}, u32[]{:S(2)}) collective-permute-start(f32[8,128]{1,0:T(8,128)S(1)} %get-tuple-element.22.refs_0_), channel_id=1, source_target_pairs={{0,2},{1,3},{2,0},{3,1},{4,6},{5,7},{6,4},{7,5},{8,10},{9,11},{10,... | collective-permute-start | bytes 12296 | tf_op jit(solution)/shard_map/ppermute | solution.py:206
  28.9 1.3 %collective-permute-start.13 = (f32[8,128]{1,0:T(8,128)S(1)}, f32[8,128]{1,0:T(8,128)S(1)}, u32[]{:S(2)}, u32[]{:S(2)}) collective-permute-start(f32[8,128]{1,0:T(8,128)S(1)} %get-tuple-element.22.refs_0_), channel_id=1, source_target_pairs={{0,3},{1,2},{2,1},{3,0},{4,7},{5,6},{6,5},{7,4},{8,11},{9,10},{10,... | collective-permute-start | bytes 12296 | tf_op jit(solution)/shard_map/ppermute | solution.py:206
  30.2 0.3 collective-permute-done.12.refs_2_
  30.5 3.8 %collective-permute-done.13.refs_3_ = f32[8,128]{1,0:T(8,128)S(1)} collective-permute-done((f32[8,128]{1,0:T(8,128)S(1)}, f32[8,128]{1,0:T(8,128)S(1)}, u32[]{:S(2)}, u32[]{:S(2)}) %collective-permute-start.13) | collective-permute-done | bytes 4128 | tf_op jit(solution)/shard_map/ppermute | solution.py:206
  34.3 0.8 %collective-permute-start.14 = (f32[8,128]{1,0:T(8,128)S(1)}, f32[8,128]{1,0:T(8,128)S(1)}, u32[]{:S(2)}, u32[]{:S(2)}) collective-permute-start(f32[8,128]{1,0:T(8,128)S(1)} %shard_map.45.refs_0_), channel_id=1, source_target_pairs={{0,8},{4,12},{8,0},{12,4},{16,24},{20,28},{24,16},{28,20},{1,9},{5... | collective-permute-start | bytes 12296 | tf_op jit(solution)/shard_map/ppermute | solution.py:210
  35.1 1.5 %collective-permute-start.15 = (f32[8,128]{1,0:T(8,128)S(1)}, f32[8,128]{1,0:T(8,128)S(1)}, u32[]{:S(2)}, u32[]{:S(2)}) collective-permute-start(f32[8,128]{1,0:T(8,128)S(1)} %shard_map.45.refs_0_), channel_id=1, source_target_pairs={{0,16},{4,20},{8,24},{12,28},{16,0},{20,4},{24,8},{28,12},{1,17},{... | collective-permute-start | bytes 12296 | tf_op jit(solution)/shard_map/ppermute | solution.py:210
  36.6 1.2 %collective-permute-start.16 = (f32[8,128]{1,0:T(8,128)S(1)}, f32[8,128]{1,0:T(8,128)S(1)}, u32[]{:S(2)}, u32[]{:S(2)}) collective-permute-start(f32[8,128]{1,0:T(8,128)S(1)} %shard_map.45.refs_0_), channel_id=1, source_target_pairs={{0,24},{4,28},{8,16},{12,20},{16,8},{20,12},{24,0},{28,4},{1,25},{... | collective-permute-start | bytes 12296 | tf_op jit(solution)/shard_map/ppermute | solution.py:210
  37.8 0.1 collective-permute-done.14.refs_1_
  37.9 0.8 %collective-permute-done.15.refs_2_ = f32[8,128]{1,0:T(8,128)S(1)} collective-permute-done((f32[8,128]{1,0:T(8,128)S(1)}, f32[8,128]{1,0:T(8,128)S(1)}, u32[]{:S(2)}, u32[]{:S(2)}) %collective-permute-start.15) | collective-permute-done | bytes 4128 | tf_op jit(solution)/shard_map/ppermute | solution.py:210
  38.7 2.4 %collective-permute-done.16.refs_3_ = f32[8,128]{1,0:T(8,128)S(1)} collective-permute-done((f32[8,128]{1,0:T(8,128)S(1)}, f32[8,128]{1,0:T(8,128)S(1)}, u32[]{:S(2)}, u32[]{:S(2)}) %collective-permute-start.16) | collective-permute-done | bytes 4128 | tf_op jit(solution)/shard_map/ppermute | solution.py:210
  41.1 1.2 %shard_map.46 = f32[8,512]{1,0:T(8,128)} custom-call(f32[8,512]{1,0:T(8,128)S(1)} %get-tuple-element.21.update_ref, f32[8,128]{1,0:T(8,128)S(1)} %shard_map.45.refs_0_, f32[8,128]{1,0:T(8,128)S(1)} %collective-permute-done.14.refs_1_, f32[8,128]{1,0:T(8,128)S(1)} %collective-permute-done.15.refs_2_, f32[8,128]{1,0:T(8,128)S(1)} %collective-permute-done.16.refs_3_), custom_call_target="tpu_custom_call" | custom-call | flops 1000000 | bytes 100000 | tf_op jit(solution)/shard_map/pallas_call | solution.py:20
  (12 shorter events, 0.0 us)
Async XLA Ops:
  0.7 7.4 %collective-permute-start = (bf16[8,1664]{1,0:T(8,128)(2,1)S(1)}, bf16[8,1664]{1,0:T(8,128)(2,1)S(1)}, u32[]{:S(2)}, u32[]{:S(2)}) collective-permute-start(bf16[8,1664]{1,0:T(8,128)(2,1)S(1)} %shard_map.37.own_ref), channel_id=1, source_target_pairs={{0,1},{1,0},{2,3},{3,2},{4,5},{5,4},{6,7},{7,6},{8,9},{9,8},{10,11... | collective-permute-start | bytes 79880 | tf_op jit(solution)/shard_map/ppermute | solution.py:206
  3.9 5.8 %collective-permute-start.3 = (bf16[8,1664]{1,0:T(8,128)(2,1)S(1)}, bf16[8,1664]{1,0:T(8,128)(2,1)S(1)}, u32[]{:S(2)}, u32[]{:S(2)}) collective-permute-start(bf16[8,1664]{1,0:T(8,128)(2,1)S(1)} %shard_map.37.own_ref), channel_id=1, source_target_pairs={{0,4},{4,0},{8,12},{12,8},{16,20},{20,16},{24,28},{28,24},{1,5},{5... | collective-permute-start | bytes 79880 | tf_op jit(solution)/shard_map/ppermute | solution.py:203
  3.9 6.3 %collective-permute-start.1 = (bf16[8,1664]{1,0:T(8,128)(2,1)S(1)}, bf16[8,1664]{1,0:T(8,128)(2,1)S(1)}, u32[]{:S(2)}, u32[]{:S(2)}) collective-permute-start(bf16[8,1664]{1,0:T(8,128)(2,1)S(1)} %shard_map.37.own_ref), channel_id=1, source_target_pairs={{0,2},{1,3},{2,0},{3,1},{4,6},{5,7},{6,4},{7,5},{8,10},{9,11},{10,... | collective-permute-start | bytes 79880 | tf_op jit(solution)/shard_map/ppermute | solution.py:206
  6.5 5.6 %collective-permute-start.2 = (bf16[8,1664]{1,0:T(8,128)(2,1)S(1)}, bf16[8,1664]{1,0:T(8,128)(2,1)S(1)}, u32[]{:S(2)}, u32[]{:S(2)}) collective-permute-start(bf16[8,1664]{1,0:T(8,128)(2,1)S(1)} %shard_map.37.own_ref), channel_id=1, source_target_pairs={{0,3},{1,2},{2,1},{3,0},{4,7},{5,6},{6,5},{7,4},{8,11},{9,10},{10,... | collective-permute-start | bytes 79880 | tf_op jit(solution)/shard_map/ppermute | solution.py:206
  6.5 8.7 %collective-permute-start.4 = (bf16[8,1664]{1,0:T(8,128)(2,1)S(1)}, bf16[8,1664]{1,0:T(8,128)(2,1)S(1)}, u32[]{:S(2)}, u32[]{:S(2)}) collective-permute-start(bf16[8,1664]{1,0:T(8,128)(2,1)S(1)} %shard_map.37.own_ref), channel_id=1, source_target_pairs={{0,8},{4,12},{8,0},{12,4},{16,24},{20,28},{24,16},{28,20},{1,9},{5... | collective-permute-start | bytes 79880 | tf_op jit(solution)/shard_map/ppermute | solution.py:210
  8.2 7.5 %collective-permute-start.5 = (bf16[8,1664]{1,0:T(8,128)(2,1)S(1)}, bf16[8,1664]{1,0:T(8,128)(2,1)S(1)}, u32[]{:S(2)}, u32[]{:S(2)}) collective-permute-start(bf16[8,1664]{1,0:T(8,128)(2,1)S(1)} %shard_map.37.own_ref), channel_id=1, source_target_pairs={{0,16},{4,20},{8,24},{12,28},{16,0},{20,4},{24,8},{28,12},{1,17},{... | collective-permute-start | bytes 79880 | tf_op jit(solution)/shard_map/ppermute | solution.py:210
  9.7 6.0 %collective-permute-start.6 = (bf16[8,1664]{1,0:T(8,128)(2,1)S(1)}, bf16[8,1664]{1,0:T(8,128)(2,1)S(1)}, u32[]{:S(2)}, u32[]{:S(2)}) collective-permute-start(bf16[8,1664]{1,0:T(8,128)(2,1)S(1)} %shard_map.37.own_ref), channel_id=1, source_target_pairs={{0,24},{4,28},{8,16},{12,20},{16,8},{20,12},{24,0},{28,4},{1,25},{... | collective-permute-start | bytes 79880 | tf_op jit(solution)/shard_map/ppermute | solution.py:210
  12.1 6.9 %collective-permute-start.7 = (bf16[8,4992]{1,0:T(8,128)(2,1)S(1)}, bf16[8,4992]{1,0:T(8,128)(2,1)S(1)}, u32[]{:S(2)}, u32[]{:S(2)}) collective-permute-start(bf16[8,4992]{1,0:T(8,128)(2,1)S(1)} %shard_map.40), channel_id=1, source_target_pairs={{0,24},{4,28},{8,16},{12,20},{16,8},{20,12},{24,0},{28,4},{1,25},{... | collective-permute-start | bytes 239624 | tf_op jit(solution)/shard_map/ppermute | solution.py:210
  14.6 6.2 %collective-permute-start.8 = (bf16[8,4992]{1,0:T(8,128)(2,1)S(1)}, bf16[8,4992]{1,0:T(8,128)(2,1)S(1)}, u32[]{:S(2)}, u32[]{:S(2)}) collective-permute-start(bf16[8,4992]{1,0:T(8,128)(2,1)S(1)} %shard_map.40), channel_id=1, source_target_pairs={{0,16},{4,20},{8,24},{12,28},{16,0},{20,4},{24,8},{28,12},{1,17},{... | collective-permute-start | bytes 239624 | tf_op jit(solution)/shard_map/ppermute | solution.py:210
  15.1 7.4 %collective-permute-start.9 = (bf16[8,4992]{1,0:T(8,128)(2,1)S(1)}, bf16[8,4992]{1,0:T(8,128)(2,1)S(1)}, u32[]{:S(2)}, u32[]{:S(2)}) collective-permute-start(bf16[8,4992]{1,0:T(8,128)(2,1)S(1)} %shard_map.40), channel_id=1, source_target_pairs={{0,8},{4,12},{8,0},{12,4},{16,24},{20,28},{24,16},{28,20},{1,9},{5... | collective-permute-start | bytes 239624 | tf_op jit(solution)/shard_map/ppermute | solution.py:210
  24.3 1.4 %collective-permute-start.10 = (f32[16,1024]{1,0:T(8,128)S(1)}, f32[16,1024]{1,0:T(8,128)S(1)}, u32[]{:S(2)}, u32[]{:S(2)}) collective-permute-start(f32[16,1024]{1,0:T(8,128)S(1)} %shard_map.43.mine_ref), channel_id=1, source_target_pairs={{0,4},{4,0},{8,12},{12,8},{16,20},{20,16},{24,28},{28,24},{1,5},{5... | collective-permute-start | bytes 196616 | tf_op jit(solution)/shard_map/ppermute | solution.py:203
  25.7 4.4 %collective-permute-start.11 = (f32[8,128]{1,0:T(8,128)S(1)}, f32[8,128]{1,0:T(8,128)S(1)}, u32[]{:S(2)}, u32[]{:S(2)}) collective-permute-start(f32[8,128]{1,0:T(8,128)S(1)} %get-tuple-element.22.refs_0_), channel_id=1, source_target_pairs={{0,1},{1,0},{2,3},{3,2},{4,5},{5,4},{6,7},{7,6},{8,9},{9,8},{10,11... | collective-permute-start | bytes 12296 | tf_op jit(solution)/shard_map/ppermute | solution.py:206
  25.8 4.7 %collective-permute-start.12 = (f32[8,128]{1,0:T(8,128)S(1)}, f32[8,128]{1,0:T(8,128)S(1)}, u32[]{:S(2)}, u32[]{:S(2)}) collective-permute-start(f32[8,128]{1,0:T(8,128)S(1)} %get-tuple-element.22.refs_0_), channel_id=1, source_target_pairs={{0,2},{1,3},{2,0},{3,1},{4,6},{5,7},{6,4},{7,5},{8,10},{9,11},{10,... | collective-permute-start | bytes 12296 | tf_op jit(solution)/shard_map/ppermute | solution.py:206
  28.9 5.4 %collective-permute-start.13 = (f32[8,128]{1,0:T(8,128)S(1)}, f32[8,128]{1,0:T(8,128)S(1)}, u32[]{:S(2)}, u32[]{:S(2)}) collective-permute-start(f32[8,128]{1,0:T(8,128)S(1)} %get-tuple-element.22.refs_0_), channel_id=1, source_target_pairs={{0,3},{1,2},{2,1},{3,0},{4,7},{5,6},{6,5},{7,4},{8,11},{9,10},{10,... | collective-permute-start | bytes 12296 | tf_op jit(solution)/shard_map/ppermute | solution.py:206
  34.3 3.6 %collective-permute-start.14 = (f32[8,128]{1,0:T(8,128)S(1)}, f32[8,128]{1,0:T(8,128)S(1)}, u32[]{:S(2)}, u32[]{:S(2)}) collective-permute-start(f32[8,128]{1,0:T(8,128)S(1)} %shard_map.45.refs_0_), channel_id=1, source_target_pairs={{0,8},{4,12},{8,0},{12,4},{16,24},{20,28},{24,16},{28,20},{1,9},{5... | collective-permute-start | bytes 12296 | tf_op jit(solution)/shard_map/ppermute | solution.py:210
  35.1 3.6 %collective-permute-start.15 = (f32[8,128]{1,0:T(8,128)S(1)}, f32[8,128]{1,0:T(8,128)S(1)}, u32[]{:S(2)}, u32[]{:S(2)}) collective-permute-start(f32[8,128]{1,0:T(8,128)S(1)} %shard_map.45.refs_0_), channel_id=1, source_target_pairs={{0,16},{4,20},{8,24},{12,28},{16,0},{20,4},{24,8},{28,12},{1,17},{... | collective-permute-start | bytes 12296 | tf_op jit(solution)/shard_map/ppermute | solution.py:210
  36.6 4.5 %collective-permute-start.16 = (f32[8,128]{1,0:T(8,128)S(1)}, f32[8,128]{1,0:T(8,128)S(1)}, u32[]{:S(2)}, u32[]{:S(2)}) collective-permute-start(f32[8,128]{1,0:T(8,128)S(1)} %shard_map.45.refs_0_), channel_id=1, source_target_pairs={{0,24},{4,28},{8,16},{12,20},{16,8},{20,12},{24,0},{28,4},{1,25},{... | collective-permute-start | bytes 12296 | tf_op jit(solution)/shard_map/ppermute | solution.py:210
where the time goes:
time: 42.5 us; the launch traced here: 42.4 us
  starting transfers between devices  20.8 us (49%)
  Pallas kernels  10.8 us (25%)
  waiting for transfers between devices  10.7 us (25%)
    pallas_call x10, Pallas kernels, call(): pl.pallas_call(kernel, out_shape=jax.tree.map(lambda s: pltpu.VMEM(s.shap...  10.8 us
    ppermute x9, starting transfers between devices, across(): lax.ppermute(x, 'row', [(2 * i + core, 2 * j + core) for i, j in enumerat...  10.5 us
    ppermute x6, starting transfers between devices, along(): lax.ppermute(x, 'col', list(enumerate(partners(n_col, step))))  10.1 us
    ppermute x6, waiting for transfers between devices, along(): lax.ppermute(x, 'col', list(enumerate(partners(n_col, step))))  6.11 us
    ppermute x9, waiting for transfers between devices, across(): lax.ppermute(x, 'row', [(2 * i + core, 2 * j + core) for i, j in enumerat...  3.36 us
    ppermute x2, waiting for transfers between devices, to_mate(): return lax.ppermute(x, 'row', [(i, i ^ 1) for i in range(n_row)])  1.24 us
  transfers between devices with their start and end apart: 17, of which 7 were waited for; matrix products, arithmetic and copies ran while one was open for 0% of the time, Pallas kernels for 17%

commit v1 on v0

--- a/solution.py
+++ b/solution.py
@@ -98,14 +98,14 @@
         full = expand(block_ref, pl.multiple_of(c * span, 128), *sizes)
         rate = 1.0 / full[dims + SCALE : dims + SCALE + 1]
         block = full.astype(BF16)
-        right = jnp.concatenate([block] * 4, axis=0)
+        right = jnp.concatenate([block] * 3, axis=0)
         for m in range(0, rows, tall):
             exponent = lax.dot_general(
-                left_ref[m : m + tall, :], right, (((1,), (0,)), ((), ())), preferred_element_type=F32
+                left_ref[m : m + tall, : right.shape[0]], right, (((1,), (0,)), ((), ())), preferred_element_type=F32
             )
             affinity = jnp.exp2(exponent * rate).astype(BF16)
             acc_ref[:, m : m + tall] += lax.dot_general(
-                block, affinity, (((1,), (1,)), ((), ())), preferred_element_type=F32
+                block[dims:], affinity, (((1,), (1,)), ((), ())), preferred_element_type=F32
             )
         return carry
 
@@ -115,16 +115,34 @@
         lax.fori_loop(0, count, step, 0, unroll=min(count, 3))
 
 
+def set_left(left_ref, at, block_refs, sizes):
+    dims, _, local = sizes
+    for ref, start in block_refs:
+        factor = left_factor(expand(ref, start, *sizes), dims)
+        left_ref[at : at + local, :] = factor.T.astype(BF16)
+        at += local
+
+
 def own_kernel(sizes, tall, own_ref, mate_ref, left_ref, acc_ref):
-    dims, _, local = sizes
-    left_ref[:local, :] = left_factor(expand(own_ref, 0, *sizes), dims).T.astype(BF16)
-    left_ref[local:, :] = left_factor(expand(mate_ref, 0, *sizes), dims).T.astype(BF16)
+    set_left(left_ref, 0, [(own_ref, 0), (mate_ref, 0)], sizes)
     acc_ref[...] = jnp.zeros_like(acc_ref)
+    accumulate(left_ref, own_ref, acc_ref, sizes, tall)
+
+
+def buddy_kernel(sizes, tall, own_ref, mate_ref, buddy_ref, upper_ref, part_ref, left_ref, acc_ref, half_ref, sum_ref):
+    rows = upper_ref.shape[0]
+    left_ref[:rows, :] = upper_ref[...]
+    acc_ref[:, :rows] = part_ref[...]
+    set_left(half_ref, 0, [(buddy_ref, 0), (buddy_ref, span_of(*sizes))], sizes)
+    left_ref[rows:, :] = half_ref[...]
+    sum_ref[...] = jnp.zeros_like(sum_ref)
 
     @pl.when(lax.axis_index("row") % 2 == 1)
     def _():
-        accumulate(left_ref, own_ref, acc_ref, sizes, tall)
-        accumulate(left_ref, mate_ref, acc_ref, sizes, tall)
+        accumulate(half_ref, own_ref, sum_ref, sizes, tall)
+        accumulate(half_ref, mate_ref, sum_ref, sizes, tall)
+
+    acc_ref[:, rows:] = sum_ref[...]
 
 
 def add_kernel(sizes, tall, left_ref, part_ref, *refs):
@@ -137,7 +155,28 @@
 def last_kernel(sizes, tall, left_ref, part_ref, *refs):
     *block_refs, out_ref, acc_ref = refs
     add_kernel(sizes, tall, left_ref, part_ref, *block_refs, acc_ref)
-    out_ref[...] = acc_ref[sizes[0] :, :]
+    write_product(out_ref, acc_ref[AUX:, :], acc_ref[ONE : ONE + 1, :])
+
+
+def write_product(out_ref, product, degree):
+    rows = product.shape[1]
+    out_ref[:, :rows] = product
+    piece = rows // AUX
+    out_ref[:, rows:] = place_rows([degree[:, i * piece : (i + 1) * piece] for i in range(AUX)], piece)
+
+
+def read_product(ref, segments):
+    rows = ref.shape[1] * AUX // (AUX + 1)
+    tail = ref[:, rows:]
+    degree = jnp.concatenate([tail[i : i + 1] for i in range(AUX)], axis=1)
+    size = rows // len(segments)
+    pick = lambda x: jnp.concatenate([x[:, i * size : (i + 1) * size] for i in segments], axis=1)
+    return pick(ref[:, :rows]), pick(degree)
+
+
+def chip_kernel(mine_ref, other_ref, out_ref):
+    mine, other = read_product(mine_ref, (0, 1, 2, 3)), read_product(other_ref, (1, 0, 3, 2))
+    write_product(out_ref, mine[0] + other[0], mine[1] + other[1])
 
 
 def join_kernel(*refs):
@@ -148,31 +187,37 @@
         at += block_ref.shape[1]
 
 
-def sum_kernel(*refs):
-    *part_refs, out_ref = refs
-    out_ref[...] = functools.reduce(lambda a, b: a + b, [ref[...] for ref in part_refs])
-
-
 def update_kernel(mine_ref, other_ref, update_ref, gram_ref):
-    local = update_ref.shape[1]
-    own = mine_ref[:, :local] + other_ref[:, local:]
-    mate = mine_ref[:, local:] + other_ref[:, :local]
-    own = own[AUX:] / own[ONE : ONE + 1]
-    mate = mate[AUX:] / mate[ONE : ONE + 1]
-    update_ref[...] = own
-    kvec = own.shape[0]
+    mine, other = read_product(mine_ref, (0, 1)), read_product(other_ref, (1, 0))
+    update = (mine[0] + other[0]) / (mine[1] + other[1])
+    update_ref[...] = update[:, : update_ref.shape[1]]
     column = lax.broadcasted_iota(jnp.int32, gram_ref.shape, 1)
     gram = jnp.zeros(gram_ref.shape, F32)
-    for k in range(kvec):
-        with_k = jnp.sum(own * own[k : k + 1] + mate * mate[k : k + 1], axis=1, keepdims=True)
-        gram = jnp.where(column == k, with_k, gram)
+    for k in range(update.shape[0]):
+        gram = jnp.where(column == k, jnp.sum(update * update[k : k + 1], axis=1, keepdims=True), gram)
     gram_ref[...] = gram
 
 
-def basis_kernel(root, update_ref, *refs):
-    *gram_refs, out_ref = refs
-    gram = functools.reduce(lambda a, b: a + b, [ref[...] for ref in gram_refs])
-    rest = update_ref[...]
+def line_kernel(update_ref, *refs):
+    *gram_refs, line_ref, out_ref = refs
+    local = update_ref.shape[1] // 2
+    line = functools.reduce(lambda a, b: a + b, [ref[...] for ref in gram_refs])
+    line_ref[...] = line
+    out_ref[:, :local] = update_ref[:, local:]
+    out_ref[:, local:] = line
+
+
+def basis_kernel(root, update_ref, line_ref, given_ref, *refs):
+    *line_refs, out_ref = refs
+    local = out_ref.shape[1]
+    odd = lax.axis_index("row") % 2 == 1
+    others = len(line_refs) // 2
+    lines = [line_ref[...], *[ref[...] for ref in line_refs[:others]]]
+    lines_given = [given_ref[:, local:], *[ref[...] for ref in line_refs[others:]]]
+    gram = functools.reduce(
+        lambda a, b: a + b, [jnp.where(odd, mine, given) for mine, given in zip(lines, lines_given)]
+    )
+    rest = jnp.where(odd, update_ref[:, :local], given_ref[:, :local])
     kvec = rest.shape[0]
     row = lax.broadcasted_iota(jnp.int32, gram.shape, 0)
     column = lax.broadcasted_iota(jnp.int32, gram.shape, 1)
@@ -197,61 +242,95 @@
     packed = dims + AUX + kvec
     sizes = (dims, kvec, local)
     span = span_of(*sizes)
-    chips = n_row // 2
 
     def to_mate(x):
         return lax.ppermute(x, "row", [(i, i ^ 1) for i in range(n_row)])
 
     def along(x):
         return [lax.ppermute(x, "col", list(enumerate(partners(n_col, step)))) for step in range(1, n_col)]
+
+    def to_buddy(x):
+        return lax.ppermute(x, "row", [(i, i ^ 2) for i in range(n_row)])
 
     def across(x):
         return [
             lax.ppermute(
-                x, "row", [(2 * i + core, 2 * j + core) for i, j in enumerate(partners(chips, step)) for core in (0, 1)]
+                x, "row", [(4 * i + k, 4 * j + k) for i, j in enumerate(partners(n_row // 4, step)) for k in range(4)]
             )
-            for step in range(1, chips)
+            for step in range(1, n_row // 4)
         ]
+
+    def odd_only(x, places, idle):
+        flat = lambda i, j: i * n_col + j
+        pairs = [
+            (flat(i, j), flat(*(places(i, j) if i % 2 else (i ^ idle, j)))) for i in range(n_row) for j in range(n_col)
+        ]
+        return lax.ppermute(x, ("row", "col"), pairs)
+
+    def odd_along(x):
+        return [odd_only(x, lambda i, j: (i, partners(n_col, step)[j]), 2) for step in range(1, n_col)]
+
+    def odd_across(x, flip):
+        others = range(1, n_row // 4)
+        place = lambda i, step: 4 * partners(n_row // 4, step)[i // 4] + (i % 4 ^ flip)
+        return [lax.ppermute(x, "row", [(i, place(i, step)) for i in range(n_row)]) for step in others]
+
+    def odd_buddy(x):
+        return odd_only(x, lambda i, j: (i ^ 2, j), 4 if n_row % 8 == 0 else 2)
 
     shape = jax.ShapeDtypeStruct
     block = call(pack_kernel, shape((AUX, span), BF16), points, spread, vectors, in_hbm=True)
+    column = along(block)
     mate = to_mate(block)
-    column = along(block)
     beside = across(block)
-
+    buddy = to_buddy(call(join_kernel, shape((AUX, 2 * span), BF16), block, mate))
+    rows = 4 * local
     tall = math.gcd(2 * local, 1024)
-
-    def size(blocks):
-        pairs = 2 * local * blocks * local
+    product = shape((kvec, rows // AUX * (AUX + 1)), F32)
+
+    def size(blocks, share=1):
+        pairs = rows // share * blocks * local
         return dict(flops=2 * 2 * pairs * 160, exps=pairs, moved=10**6)
 
     left, part = call(
         functools.partial(own_kernel, sizes, tall),
-        (shape((2 * local, 4 * packed), BF16), shape((packed, 2 * local), F32)),
-        block, mate, **size(1),
+        (shape((rows // 2, 4 * packed), BF16), shape((packed - dims, rows // 2), F32)),
+        block, mate, **size(1, 2),
     )
     column, left, part = lax.optimization_barrier((column, left, part))
     joined = call(join_kernel, shape((AUX, span * (n_col - 1)), BF16), *column)
     far = across(joined)
-    near = [*column, *beside]
+    left, part = call(
+        functools.partial(buddy_kernel, sizes, tall),
+        (shape((rows, 4 * packed), BF16), shape((packed - dims, rows), F32)),
+        block, mate, buddy, left, part,
+        scratch=[pltpu.VMEM((rows // 2, 4 * packed), BF16), pltpu.VMEM((packed - dims, rows // 2), F32)],
+        **size(1, 2),
+    )
     part = call(
         functools.partial(add_kernel, sizes, tall),
-        shape((packed, 2 * local), F32), left, part, *near, **size(len(near)),
-    )
-    for index, block in enumerate(far[::-1]):
-        final = index == len(far) - 1
-        part = call(
-            functools.partial(last_kernel if final else add_kernel, sizes, tall),
-            shape((packed - dims if final else packed, 2 * local), F32),
-            left, part, block,
-            scratch=[pltpu.VMEM((packed, 2 * local), F32)] * final,
-            **size(n_col - 1),
-        )
-    update, gram = call(update_kernel, (shape((kvec, local), F32), shape((kvec, 128), F32)), part, to_mate(part))
-    gram = call(sum_kernel, shape(gram.shape, F32), gram, *along(gram))
+        shape((packed - dims, rows), F32), left, part, *column, **size(len(column)),
+    )
+    rest = [*beside, *far[::-1]]
+    part = call(
+        functools.partial(last_kernel, sizes, tall),
+        product, left, part, *rest,
+        scratch=[pltpu.VMEM((packed - dims, rows), F32)], **size(len(beside) + len(far) * (n_col - 1)),
+    )
+    chip = call(chip_kernel, product, part, to_mate(part))
+    update, gram = call(update_kernel, (shape((kvec, 2 * local), F32), shape((kvec, 128), F32)), chip, odd_buddy(chip))
+    line, given = call(
+        line_kernel,
+        (shape(gram.shape, F32), shape((kvec, local + 128), F32)),
+        update, gram, *odd_along(gram),
+    )
+    lines = [*odd_across(line, 0), *odd_across(line, 1)]
     root = math.sqrt(local * n_row * n_col)
     return call(
-        functools.partial(basis_kernel, root), shape((kvec, local), F32), update, gram, *across(gram), out_vmem=False
+        functools.partial(basis_kernel, root),
+        shape((kvec, local), F32),
+        update, line, to_mate(given), *lines,
+        out_vmem=False,
     )
 
 

time: 42.5 us -> 41 us (0.965)
  starting transfers between devices: 20.8 us -> 16.5 us
  waiting for transfers between devices: 10.7 us -> 14 us
    ppermute x6 -> x3, starting transfers between devices: 10.1 us -> 4.39 us  [along(): lax.ppermute(x, 'col', list(enumerate(partners(n_col, step))))]
    ppermute x9, waiting for transfers between devices: 3.36 us -> 8.68 us  [the longest x4 6.37 us: odd_only(): return lax.ppermute(x, ('row', 'col'), pairs)]
    ppermute x6 -> x3, waiting for transfers between devices: 6.11 us -> 3.17 us  [along(): lax.ppermute(x, 'col', list(enumerate(partners(n_col, step))))]
    ppermute x9, starting transfers between devices: 10.5 us -> 11.5 us  [the longest x4 3.71 us: odd_only(): return lax.ppermute(x, ('row', 'col'), pairs)]
    ppermute x2 -> x3, waiting for transfers between devices: 1.24 us -> 2.11 us  [to_mate(): return lax.ppermute(x, 'row', [(i, i ^ 1) for i in range(n_row)])]
    ppermute x2 -> x3, starting transfers between devices: 0.12 us -> 0.63 us  [to_mate(): return lax.ppermute(x, 'row', [(i, i ^ 1) for i in range(n_row)])]
    pallas_call x10 -> x11, Pallas kernels: 10.8 us -> 10.4 us  [call(): pl.pallas_call(kernel, out_shape=jax.tree.map(lambda s: pltpu.VMEM(s.shap...]
  transfers between devices with their start and end apart: 17 -> 15, of which waited for: 7 -> 10; matrix products, arithmetic and copies ran while one was open for 0% -> 0% of each run, Pallas kernels for 17% -> 10%
where the time goes in v1:
time: 41 us; the launch traced here: 40.9 us
  starting transfers between devices  16.5 us (40%)
  waiting for transfers between devices  14 us (34%)
  Pallas kernels  10.4 us (25%)
    pallas_call x11, Pallas kernels, call(): pl.pallas_call(kernel, out_shape=jax.tree.map(lambda s: pltpu.VMEM(s.shap...  10.4 us
    ppermute x4, waiting for transfers between devices, odd_only(): return lax.ppermute(x, ('row', 'col'), pairs)  6.37 us
    ppermute x3, starting transfers between devices, along(): lax.ppermute(x, 'col', list(enumerate(partners(n_col, step))))  4.39 us
    ppermute x4, starting transfers between devices, odd_only(): return lax.ppermute(x, ('row', 'col'), pairs)  3.71 us
    ppermute x3, waiting for transfers between devices, along(): lax.ppermute(x, 'col', list(enumerate(partners(n_col, step))))  3.17 us
    ppermute x2, starting transfers between devices, across(): lax.ppermute(x, 'row', [(4 * i + k, 4 * j + k) for i, j in enumerate(part...  3.1 us
    ppermute x1, starting transfers between devices, to_buddy(): return lax.ppermute(x, 'row', [(i, i ^ 2) for i in range(n_row)])  2.82 us
    ppermute x2, waiting for transfers between devices, odd_across(): lax.ppermute(x, 'row', [(i, place(i, step)) for i in range(n_row)])  2.3 us
  transfers between devices with their start and end apart: 15, of which 10 were waited for; matrix products, arithmetic and copies ran while one was open for 0% of the time, Pallas kernels for 10%

profile of v1, /device:TPU:0, one launch (start us, length us, event | category | flops | bytes accessed | tf_op | source)
XLA Modules:
  0.0 40.9 jit_solution(4237872643364718092)
XLA Ops:
  0.0 0.7 %shard_map.37.refs_0_.own_ref = bf16[8,1664]{1,0:T(8,128)(2,1)S(1)} custom-call(bf16[16,512]{1,0:T(8,128)(2,1)} %points_ref.1, bf16[512]{0:T(512)(128)(2,1)} %spread_ref.1, bf16[8,512]{1,0:T(8,128)(2,1)} %vectors_ref.1), custom_call_target="tpu_custom_call" | custom-call | flops 1000000 | bytes 100000 | tf_op jit(solution)/shard_map/pallas_call | solution.py:20
  0.7 0.6 %collective-permute-start = (bf16[8,1664]{1,0:T(8,128)(2,1)S(1)}, bf16[8,1664]{1,0:T(8,128)(2,1)S(1)}, u32[]{:S(2)}, u32[]{:S(2)}) collective-permute-start(bf16[8,1664]{1,0:T(8,128)(2,1)S(1)} %shard_map.37.refs_0_.own_ref), channel_id=1, source_target_pairs={{0,4},{4,0},{8,12},{12,8},{16,20},{20,16},{24,28},{28,24},{1,5},{5... | collective-permute-start | bytes 79880 | tf_op jit(solution)/shard_map/ppermute | solution.py:247
  1.3 0.9 %collective-permute-done.refs_1_.mate_ref = bf16[8,1664]{1,0:T(8,128)(2,1)S(1)} collective-permute-done((bf16[8,1664]{1,0:T(8,128)(2,1)S(1)}, bf16[8,1664]{1,0:T(8,128)(2,1)S(1)}, u32[]{:S(2)}, u32[]{:S(2)}) %collective-permute-start) | collective-permute-done | bytes 26656 | tf_op jit(solution)/shard_map/ppermute | solution.py:247
  2.2 2.8 %collective-permute-start.1 = (bf16[8,3328]{1,0:T(8,128)(2,1)S(1)}, bf16[8,3328]{1,0:T(8,128)(2,1)S(1)}, u32[]{:S(2)}, u32[]{:S(2)}) collective-permute-start(bf16[8,3328]{1,0:T(8,128)(2,1)S(1)} %shard_map.38), channel_id=1, source_target_pairs={{0,8},{4,12},{8,0},{12,4},{16,24},{20,28},{24,16},{28,20},{1,9},{5... | collective-permute-start | bytes 159752 | tf_op jit(solution)/shard_map/ppermute | solution.py:253
  5.0 1.6 %collective-permute-start.2 = (bf16[8,1664]{1,0:T(8,128)(2,1)S(1)}, bf16[8,1664]{1,0:T(8,128)(2,1)S(1)}, u32[]{:S(2)}, u32[]{:S(2)}) collective-permute-start(bf16[8,1664]{1,0:T(8,128)(2,1)S(1)} %shard_map.37.refs_0_.own_ref), channel_id=1, source_target_pairs={{0,1},{1,0},{2,3},{3,2},{4,5},{5,4},{6,7},{7,6},{8,9},{9,8},{10,11... | collective-permute-start | bytes 79880 | tf_op jit(solution)/shard_map/ppermute | solution.py:250
  6.6 2.6 %collective-permute-start.3 = (bf16[8,1664]{1,0:T(8,128)(2,1)S(1)}, bf16[8,1664]{1,0:T(8,128)(2,1)S(1)}, u32[]{:S(2)}, u32[]{:S(2)}) collective-permute-start(bf16[8,1664]{1,0:T(8,128)(2,1)S(1)} %shard_map.37.refs_0_.own_ref), channel_id=1, source_target_pairs={{0,2},{1,3},{2,0},{3,1},{4,6},{5,7},{6,4},{7,5},{8,10},{9,11},{10,... | collective-permute-start | bytes 79880 | tf_op jit(solution)/shard_map/ppermute | solution.py:250
  9.2 0.2 collective-permute-start.4
  9.4 1.5 %collective-permute-start.5 = (bf16[8,1664]{1,0:T(8,128)(2,1)S(1)}, bf16[8,1664]{1,0:T(8,128)(2,1)S(1)}, u32[]{:S(2)}, u32[]{:S(2)}) collective-permute-start(bf16[8,1664]{1,0:T(8,128)(2,1)S(1)} %shard_map.37.refs_0_.own_ref), channel_id=1, source_target_pairs={{0,16},{4,20},{8,24},{12,28},{16,0},{20,4},{24,8},{28,12},{1,17},{... | collective-permute-start | bytes 79880 | tf_op jit(solution)/shard_map/ppermute | solution.py:257
  10.9 0.7 %shard_map.39 = (bf16[1024,128]{1,0:T(8,128)(2,1)S(1)}, f32[16,1024]{1,0:T(8,128)S(1)}) custom-call(bf16[8,1664]{1,0:T(8,128)(2,1)S(1)} %shard_map.37.refs_0_.own_ref, bf16[8,1664]{1,0:T(8,128)(2,1)S(1)} %collective-permute-done.refs_1_.mate_ref), custom_call_target="tpu_custom_call" | custom-call | flops 335544320 | bytes 1000000 | tf_op jit(solution)/shard_map/pallas_call | solution.py:20
  11.6 0.1 collective-permute-done.3.refs_1_
  11.8 3.0 %collective-permute-done.4.refs_2_ = bf16[8,1664]{1,0:T(8,128)(2,1)S(1)} collective-permute-done((bf16[8,1664]{1,0:T(8,128)(2,1)S(1)}, bf16[8,1664]{1,0:T(8,128)(2,1)S(1)}, u32[]{:S(2)}, u32[]{:S(2)}) %collective-permute-start.4) | collective-permute-done | bytes 26656 | tf_op jit(solution)/shard_map/ppermute | solution.py:250
  14.8 1.6 %collective-permute-start.6 = (bf16[8,4992]{1,0:T(8,128)(2,1)S(1)}, bf16[8,4992]{1,0:T(8,128)(2,1)S(1)}, u32[]{:S(2)}, u32[]{:S(2)}) collective-permute-start(bf16[8,4992]{1,0:T(8,128)(2,1)S(1)} %shard_map.42), channel_id=1, source_target_pairs={{0,16},{4,20},{8,24},{12,28},{16,0},{20,4},{24,8},{28,12},{1,17},{... | collective-permute-start | bytes 239624 | tf_op jit(solution)/shard_map/ppermute | solution.py:257
  16.4 0.2 shard_map.40
  16.6 3.1 %shard_map.41.part_ref = f32[16,2048]{1,0:T(8,128)S(1)} custom-call(bf16[2048,128]{1,0:T(8,128)(2,1)S(1)} %get-tuple-element.22.left_ref, f32[16,2048]{1,0:T(8,128)S(1)} %get-tuple-element.23.part_ref, bf16[8,1664]{1,0:T(8,128)(2,1)S(1)} %collective-permute-done.2.refs_0_, bf16[8,1664]{1,0:T(8,128)(2,1)S(1)} %collective-permute-done.3.refs_1_, ...), custom_call_target="tpu_custom_call" | custom-call | flops 2013265920 | bytes 1000000 | tf_op jit(solution)/shard_map/pallas_call | solution.py:20
  19.7 0.0 collective-permute-done.5.refs_0_
  19.7 4.1 %shard_map.43.mine_ref = f32[8,2304]{1,0:T(8,128)S(1)} custom-call(bf16[2048,128]{1,0:T(8,128)(2,1)S(1)} %get-tuple-element.22.left_ref, f32[16,2048]{1,0:T(8,128)S(1)} %shard_map.41.part_ref, bf16[8,1664]{1,0:T(8,128)(2,1)S(1)} %collective-permute-done.5.refs_0_, bf16[8,4992]{1,0:T(8,128)(2,1)S(1)} %collective-permute-done.6.refs_1_), custom_call_target="tpu_custom_call" | custom-call | flops 2684354560 | bytes 1000000 | tf_op jit(solution)/shard_map/pallas_call | solution.py:20
  23.9 0.1 collective-permute-start.7
  24.0 1.3 %collective-permute-done.7.other_ref = f32[8,2304]{1,0:T(8,128)S(1)} collective-permute-done((f32[8,2304]{1,0:T(8,128)S(1)}, f32[8,2304]{1,0:T(8,128)S(1)}, u32[]{:S(2)}, u32[]{:S(2)}) %collective-permute-start.7) | collective-permute-done | bytes 73760 | tf_op jit(solution)/shard_map/ppermute | solution.py:247
  25.2 1.1 %collective-permute-start.8 = (f32[8,2304]{1,0:T(8,128)S(1)}, f32[8,2304]{1,0:T(8,128)S(1)}, u32[]{:S(2)}, u32[]{:S(2)}) collective-permute-start(f32[8,2304]{1,0:T(8,128)S(1)} %shard_map.44.mine_ref), channel_id=1, source_target_pairs={{0,16},{1,17},{2,18},{3,19},{4,12},{5,13},{6,14},{7,15},{8,24},{9,... | collective-permute-start | bytes 221192 | tf_op jit(solution)/shard_map/ppermute | solution.py:268
  26.4 3.3 %collective-permute-done.8.other_ref = f32[8,2304]{1,0:T(8,128)S(1)} collective-permute-done((f32[8,2304]{1,0:T(8,128)S(1)}, f32[8,2304]{1,0:T(8,128)S(1)}, u32[]{:S(2)}, u32[]{:S(2)}) %collective-permute-start.8) | collective-permute-done | bytes 73760 | tf_op jit(solution)/shard_map/ppermute | solution.py:268
  29.7 0.1 shard_map.45
  29.8 0.6 %collective-permute-start.9 = (f32[8,128]{1,0:T(8,128)S(1)}, f32[8,128]{1,0:T(8,128)S(1)}, u32[]{:S(2)}, u32[]{:S(2)}) collective-permute-start(f32[8,128]{1,0:T(8,128)S(1)} %get-tuple-element.28.refs_0_), channel_id=1, source_target_pairs={{0,8},{1,9},{2,10},{3,11},{4,5},{5,4},{6,7},{7,6},{8,0},{9,1},{10,... | collective-permute-start | bytes 12296 | tf_op jit(solution)/shard_map/ppermute | solution.py:268
  30.4 1.5 %collective-permute-start.10 = (f32[8,128]{1,0:T(8,128)S(1)}, f32[8,128]{1,0:T(8,128)S(1)}, u32[]{:S(2)}, u32[]{:S(2)}) collective-permute-start(f32[8,128]{1,0:T(8,128)S(1)} %get-tuple-element.28.refs_0_), channel_id=1, source_target_pairs={{0,8},{1,9},{2,10},{3,11},{4,6},{5,7},{6,4},{7,5},{8,0},{9,1},{10,... | collective-permute-start | bytes 12296 | tf_op jit(solution)/shard_map/ppermute | solution.py:268
  31.9 0.5 %collective-permute-start.11 = (f32[8,128]{1,0:T(8,128)S(1)}, f32[8,128]{1,0:T(8,128)S(1)}, u32[]{:S(2)}, u32[]{:S(2)}) collective-permute-start(f32[8,128]{1,0:T(8,128)S(1)} %get-tuple-element.28.refs_0_), channel_id=1, source_target_pairs={{0,8},{1,9},{2,10},{3,11},{4,7},{5,6},{6,5},{7,4},{8,0},{9,1},{10,... | collective-permute-start | bytes 12296 | tf_op jit(solution)/shard_map/ppermute | solution.py:268
  32.4 1.0 %collective-permute-done.9.refs_1_ = f32[8,128]{1,0:T(8,128)S(1)} collective-permute-done((f32[8,128]{1,0:T(8,128)S(1)}, f32[8,128]{1,0:T(8,128)S(1)}, u32[]{:S(2)}, u32[]{:S(2)}) %collective-permute-start.9) | collective-permute-done | bytes 4128 | tf_op jit(solution)/shard_map/ppermute | solution.py:268
  33.4 0.5 %collective-permute-done.10.refs_2_ = f32[8,128]{1,0:T(8,128)S(1)} collective-permute-done((f32[8,128]{1,0:T(8,128)S(1)}, f32[8,128]{1,0:T(8,128)S(1)}, u32[]{:S(2)}, u32[]{:S(2)}) %collective-permute-start.10) | collective-permute-done | bytes 4128 | tf_op jit(solution)/shard_map/ppermute | solution.py:268
  34.0 1.5 %collective-permute-done.11.refs_3_ = f32[8,128]{1,0:T(8,128)S(1)} collective-permute-done((f32[8,128]{1,0:T(8,128)S(1)}, f32[8,128]{1,0:T(8,128)S(1)}, u32[]{:S(2)}, u32[]{:S(2)}) %collective-permute-start.11) | collective-permute-done | bytes 4128 | tf_op jit(solution)/shard_map/ppermute | solution.py:268
  35.5 1.1 %collective-permute-start.13 = (f32[8,128]{1,0:T(8,128)S(1)}, f32[8,128]{1,0:T(8,128)S(1)}, u32[]{:S(2)}, u32[]{:S(2)}) collective-permute-start(f32[8,128]{1,0:T(8,128)S(1)} %get-tuple-element.29.line_ref), channel_id=1, source_target_pairs={{0,16},{4,20},{8,24},{12,28},{16,0},{20,4},{24,8},{28,12},{1,17},{... | collective-permute-start | bytes 12296 | tf_op jit(solution)/shard_map/ppermute | solution.py:276
  36.6 0.7 %collective-permute-start.14 = (f32[8,128]{1,0:T(8,128)S(1)}, f32[8,128]{1,0:T(8,128)S(1)}, u32[]{:S(2)}, u32[]{:S(2)}) collective-permute-start(f32[8,128]{1,0:T(8,128)S(1)} %get-tuple-element.29.line_ref), channel_id=1, source_target_pairs={{0,20},{4,16},{8,28},{12,24},{16,4},{20,0},{24,12},{28,8},{1,21},{... | collective-permute-start | bytes 12296 | tf_op jit(solution)/shard_map/ppermute | solution.py:276
  37.3 1.8 %collective-permute-done.13.refs_0_ = f32[8,128]{1,0:T(8,128)S(1)} collective-permute-done((f32[8,128]{1,0:T(8,128)S(1)}, f32[8,128]{1,0:T(8,128)S(1)}, u32[]{:S(2)}, u32[]{:S(2)}) %collective-permute-start.13) | collective-permute-done | bytes 4128 | tf_op jit(solution)/shard_map/ppermute | solution.py:276
  39.1 0.5 %collective-permute-done.14.refs_1_ = f32[8,128]{1,0:T(8,128)S(1)} collective-permute-done((f32[8,128]{1,0:T(8,128)S(1)}, f32[8,128]{1,0:T(8,128)S(1)}, u32[]{:S(2)}, u32[]{:S(2)}) %collective-permute-start.14) | collective-permute-done | bytes 4128 | tf_op jit(solution)/shard_map/ppermute | solution.py:276
  39.6 1.3 %shard_map.47 = f32[8,512]{1,0:T(8,128)} custom-call(f32[8,1024]{1,0:T(8,128)S(1)} %get-tuple-element.27.update_ref, f32[8,128]{1,0:T(8,128)S(1)} %get-tuple-element.29.line_ref, f32[8,640]{1,0:T(8,128)S(1)} %collective-permute-done.12.given_ref, f32[8,128]{1,0:T(8,128)S(1)} %collective-permute-done.13.refs_0_, f32[8,128]{1,0:T(8,128)S(1)} %collective-permute-done.14.refs_1_), custom_call_target="tpu_custom_call" | custom-call | flops 1000000 | bytes 100000 | tf_op jit(solution)/shard_map/pallas_call | solution.py:20
  (9 shorter events, 0.1 us)
Async XLA Ops:
  0.7 1.4 %collective-permute-start = (bf16[8,1664]{1,0:T(8,128)(2,1)S(1)}, bf16[8,1664]{1,0:T(8,128)(2,1)S(1)}, u32[]{:S(2)}, u32[]{:S(2)}) collective-permute-start(bf16[8,1664]{1,0:T(8,128)(2,1)S(1)} %shard_map.37.refs_0_.own_ref), channel_id=1, source_target_pairs={{0,4},{4,0},{8,12},{12,8},{16,20},{20,16},{24,28},{28,24},{1,5},{5... | collective-permute-start | bytes 79880 | tf_op jit(solution)/shard_map/ppermute | solution.py:247
  2.2 14.2 %collective-permute-start.1 = (bf16[8,3328]{1,0:T(8,128)(2,1)S(1)}, bf16[8,3328]{1,0:T(8,128)(2,1)S(1)}, u32[]{:S(2)}, u32[]{:S(2)}) collective-permute-start(bf16[8,3328]{1,0:T(8,128)(2,1)S(1)} %shard_map.38), channel_id=1, source_target_pairs={{0,8},{4,12},{8,0},{12,4},{16,24},{20,28},{24,16},{28,20},{1,9},{5... | collective-permute-start | bytes 159752 | tf_op jit(solution)/shard_map/ppermute | solution.py:253
  5.0 6.6 %collective-permute-start.2 = (bf16[8,1664]{1,0:T(8,128)(2,1)S(1)}, bf16[8,1664]{1,0:T(8,128)(2,1)S(1)}, u32[]{:S(2)}, u32[]{:S(2)}) collective-permute-start(bf16[8,1664]{1,0:T(8,128)(2,1)S(1)} %shard_map.37.refs_0_.own_ref), channel_id=1, source_target_pairs={{0,1},{1,0},{2,3},{3,2},{4,5},{5,4},{6,7},{7,6},{8,9},{9,8},{10,11... | collective-permute-start | bytes 79880 | tf_op jit(solution)/shard_map/ppermute | solution.py:250
  6.6 5.2 %collective-permute-start.3 = (bf16[8,1664]{1,0:T(8,128)(2,1)S(1)}, bf16[8,1664]{1,0:T(8,128)(2,1)S(1)}, u32[]{:S(2)}, u32[]{:S(2)}) collective-permute-start(bf16[8,1664]{1,0:T(8,128)(2,1)S(1)} %shard_map.37.refs_0_.own_ref), channel_id=1, source_target_pairs={{0,2},{1,3},{2,0},{3,1},{4,6},{5,7},{6,4},{7,5},{8,10},{9,11},{10,... | collective-permute-start | bytes 79880 | tf_op jit(solution)/shard_map/ppermute | solution.py:250
  9.2 5.6 %collective-permute-start.4 = (bf16[8,1664]{1,0:T(8,128)(2,1)S(1)}, bf16[8,1664]{1,0:T(8,128)(2,1)S(1)}, u32[]{:S(2)}, u32[]{:S(2)}) collective-permute-start(bf16[8,1664]{1,0:T(8,128)(2,1)S(1)} %shard_map.37.refs_0_.own_ref), channel_id=1, source_target_pairs={{0,3},{1,2},{2,1},{3,0},{4,7},{5,6},{6,5},{7,4},{8,11},{9,10},{10,... | collective-permute-start | bytes 79880 | tf_op jit(solution)/shard_map/ppermute | solution.py:250
  9.4 10.4 %collective-permute-start.5 = (bf16[8,1664]{1,0:T(8,128)(2,1)S(1)}, bf16[8,1664]{1,0:T(8,128)(2,1)S(1)}, u32[]{:S(2)}, u32[]{:S(2)}) collective-permute-start(bf16[8,1664]{1,0:T(8,128)(2,1)S(1)} %shard_map.37.refs_0_.own_ref), channel_id=1, source_target_pairs={{0,16},{4,20},{8,24},{12,28},{16,0},{20,4},{24,8},{28,12},{1,17},{... | collective-permute-start | bytes 79880 | tf_op jit(solution)/shard_map/ppermute | solution.py:257
  14.8 4.9 %collective-permute-start.6 = (bf16[8,4992]{1,0:T(8,128)(2,1)S(1)}, bf16[8,4992]{1,0:T(8,128)(2,1)S(1)}, u32[]{:S(2)}, u32[]{:S(2)}) collective-permute-start(bf16[8,4992]{1,0:T(8,128)(2,1)S(1)} %shard_map.42), channel_id=1, source_target_pairs={{0,16},{4,20},{8,24},{12,28},{16,0},{20,4},{24,8},{28,12},{1,17},{... | collective-permute-start | bytes 239624 | tf_op jit(solution)/shard_map/ppermute | solution.py:257
  23.9 1.3 %collective-permute-start.7 = (f32[8,2304]{1,0:T(8,128)S(1)}, f32[8,2304]{1,0:T(8,128)S(1)}, u32[]{:S(2)}, u32[]{:S(2)}) collective-permute-start(f32[8,2304]{1,0:T(8,128)S(1)} %shard_map.43.mine_ref), channel_id=1, source_target_pairs={{0,4},{4,0},{8,12},{12,8},{16,20},{20,16},{24,28},{28,24},{1,5},{5... | collective-permute-start | bytes 221192 | tf_op jit(solution)/shard_map/ppermute | solution.py:247
  25.2 4.4 %collective-permute-start.8 = (f32[8,2304]{1,0:T(8,128)S(1)}, f32[8,2304]{1,0:T(8,128)S(1)}, u32[]{:S(2)}, u32[]{:S(2)}) collective-permute-start(f32[8,2304]{1,0:T(8,128)S(1)} %shard_map.44.mine_ref), channel_id=1, source_target_pairs={{0,16},{1,17},{2,18},{3,19},{4,12},{5,13},{6,14},{7,15},{8,24},{9,... | collective-permute-start | bytes 221192 | tf_op jit(solution)/shard_map/ppermute | solution.py:268
  29.8 3.6 %collective-permute-start.9 = (f32[8,128]{1,0:T(8,128)S(1)}, f32[8,128]{1,0:T(8,128)S(1)}, u32[]{:S(2)}, u32[]{:S(2)}) collective-permute-start(f32[8,128]{1,0:T(8,128)S(1)} %get-tuple-element.28.refs_0_), channel_id=1, source_target_pairs={{0,8},{1,9},{2,10},{3,11},{4,5},{5,4},{6,7},{7,6},{8,0},{9,1},{10,... | collective-permute-start | bytes 12296 | tf_op jit(solution)/shard_map/ppermute | solution.py:268
  30.4 3.6 %collective-permute-start.10 = (f32[8,128]{1,0:T(8,128)S(1)}, f32[8,128]{1,0:T(8,128)S(1)}, u32[]{:S(2)}, u32[]{:S(2)}) collective-permute-start(f32[8,128]{1,0:T(8,128)S(1)} %get-tuple-element.28.refs_0_), channel_id=1, source_target_pairs={{0,8},{1,9},{2,10},{3,11},{4,6},{5,7},{6,4},{7,5},{8,0},{9,1},{10,... | collective-permute-start | bytes 12296 | tf_op jit(solution)/shard_map/ppermute | solution.py:268
  31.9 3.6 %collective-permute-start.11 = (f32[8,128]{1,0:T(8,128)S(1)}, f32[8,128]{1,0:T(8,128)S(1)}, u32[]{:S(2)}, u32[]{:S(2)}) collective-permute-start(f32[8,128]{1,0:T(8,128)S(1)} %get-tuple-element.28.refs_0_), channel_id=1, source_target_pairs={{0,8},{1,9},{2,10},{3,11},{4,7},{5,6},{6,5},{7,4},{8,0},{9,1},{10,... | collective-permute-start | bytes 12296 | tf_op jit(solution)/shard_map/ppermute | solution.py:268
  35.5 4.2 %collective-permute-start.12 = (f32[8,640]{1,0:T(8,128)S(1)}, f32[8,640]{1,0:T(8,128)S(1)}, u32[]{:S(2)}, u32[]{:S(2)}) collective-permute-start(f32[8,640]{1,0:T(8,128)S(1)} %get-tuple-element.30), channel_id=1, source_target_pairs={{0,4},{4,0},{8,12},{12,8},{16,20},{20,16},{24,28},{28,24},{1,5},{5... | collective-permute-start | bytes 61448 | tf_op jit(solution)/shard_map/ppermute | solution.py:247
  35.5 3.7 %collective-permute-start.13 = (f32[8,128]{1,0:T(8,128)S(1)}, f32[8,128]{1,0:T(8,128)S(1)}, u32[]{:S(2)}, u32[]{:S(2)}) collective-permute-start(f32[8,128]{1,0:T(8,128)S(1)} %get-tuple-element.29.line_ref), channel_id=1, source_target_pairs={{0,16},{4,20},{8,24},{12,28},{16,0},{20,4},{24,8},{28,12},{1,17},{... | collective-permute-start | bytes 12296 | tf_op jit(solution)/shard_map/ppermute | solution.py:276
  36.6 3.0 %collective-permute-start.14 = (f32[8,128]{1,0:T(8,128)S(1)}, f32[8,128]{1,0:T(8,128)S(1)}, u32[]{:S(2)}, u32[]{:S(2)}) collective-permute-start(f32[8,128]{1,0:T(8,128)S(1)} %get-tuple-element.29.line_ref), channel_id=1, source_target_pairs={{0,20},{4,16},{8,28},{12,24},{16,4},{20,0},{24,12},{28,8},{1,21},{... | collective-permute-start | bytes 12296 | tf_op jit(solution)/shard_map/ppermute | solution.py:276

commit v2 on v1

--- a/solution.py
+++ b/solution.py
@@ -85,28 +85,26 @@
     factor = jnp.concatenate(
         [2 * rate * rows[:dims], aux, jnp.zeros((rows.shape[0] - dims - AUX, rows.shape[1]), F32)], axis=0
     )
-    parts = three_parts(factor)
-    return jnp.concatenate([*parts, jnp.zeros_like(factor)], axis=0)
-
-
-def accumulate(left_ref, block_ref, acc_ref, sizes, tall):
-    dims, _, _ = sizes
-    rows, span = left_ref.shape[0], span_of(*sizes)
+    return jnp.concatenate(three_parts(factor), axis=0)
+
+
+def accumulate(left_ref, block_ref, acc_ref, sizes, tall, top=0):
+    dims, _, local = sizes
+    rows, span = left_ref.shape[1], span_of(*sizes)
     count = block_ref.shape[1] // span
 
     def step(c, carry):
         full = expand(block_ref, pl.multiple_of(c * span, 128), *sizes)
         rate = 1.0 / full[dims + SCALE : dims + SCALE + 1]
-        block = full.astype(BF16)
-        right = jnp.concatenate([block] * 3, axis=0)
-        for m in range(0, rows, tall):
-            exponent = lax.dot_general(
-                left_ref[m : m + tall, : right.shape[0]], right, (((1,), (0,)), ((), ())), preferred_element_type=F32
-            )
+        depth = 3 * full.shape[0]
+        turned = jnp.concatenate([full] * 3 + [jnp.broadcast_to(rate, (128 - depth, local))], axis=0).T
+        right = turned[:, :depth].astype(BF16)
+        rate = jnp.concatenate([jnp.broadcast_to(turned[:, depth : depth + 1], (local, 128))] * (tall // 128), axis=1)
+        block = full[dims:].astype(BF16)
+        for m in range(top, rows, tall):
+            exponent = jnp.dot(right, left_ref[:, m : m + tall], preferred_element_type=F32)
             affinity = jnp.exp2(exponent * rate).astype(BF16)
-            acc_ref[:, m : m + tall] += lax.dot_general(
-                block[dims:], affinity, (((1,), (1,)), ((), ())), preferred_element_type=F32
-            )
+            acc_ref[:, m : m + tall] += jnp.dot(block, affinity, preferred_element_type=F32)
         return carry
 
     if count == 1:
@@ -119,7 +117,7 @@
     dims, _, local = sizes
     for ref, start in block_refs:
         factor = left_factor(expand(ref, start, *sizes), dims)
-        left_ref[at : at + local, :] = factor.T.astype(BF16)
+        left_ref[:, at : at + local] = factor.astype(BF16)
         at += local
 
 
@@ -130,11 +128,11 @@
 
 
 def buddy_kernel(sizes, tall, own_ref, mate_ref, buddy_ref, upper_ref, part_ref, left_ref, acc_ref, half_ref, sum_ref):
-    rows = upper_ref.shape[0]
-    left_ref[:rows, :] = upper_ref[...]
+    rows = upper_ref.shape[1]
+    left_ref[:, :rows] = upper_ref[...]
     acc_ref[:, :rows] = part_ref[...]
     set_left(half_ref, 0, [(buddy_ref, 0), (buddy_ref, span_of(*sizes))], sizes)
-    left_ref[rows:, :] = half_ref[...]
+    left_ref[:, rows:] = half_ref[...]
     sum_ref[...] = jnp.zeros_like(sum_ref)
 
     @pl.when(lax.axis_index("row") % 2 == 1)
@@ -150,6 +148,12 @@
     acc_ref[...] = part_ref[...]
     for block_ref in block_refs:
         accumulate(left_ref, block_ref, acc_ref, sizes, tall)
+
+
+def near_kernel(sizes, tall, left_ref, part_ref, early_ref, *refs):
+    *block_refs, acc_ref = refs
+    add_kernel(sizes, tall, left_ref, part_ref, *block_refs, acc_ref)
+    accumulate(left_ref, early_ref, acc_ref, sizes, tall, left_ref.shape[1] // 2)
 
 
 def last_kernel(sizes, tall, left_ref, part_ref, *refs):
@@ -294,28 +298,37 @@
 
     left, part = call(
         functools.partial(own_kernel, sizes, tall),
-        (shape((rows // 2, 4 * packed), BF16), shape((packed - dims, rows // 2), F32)),
+        (shape((3 * packed, rows // 2), BF16), shape((packed - dims, rows // 2), F32)),
         block, mate, **size(1, 2),
     )
-    column, left, part = lax.optimization_barrier((column, left, part))
-    joined = call(join_kernel, shape((AUX, span * (n_col - 1)), BF16), *column)
+    middle = n_col // 2 - 1
+    early, later = column[middle], column[:middle] + column[middle + 1 :]
+    part = call(
+        functools.partial(add_kernel, sizes, tall),
+        shape((packed - dims, rows // 2), F32), left, part, early, **size(1, 2),
+    )
+    later, left, part = lax.optimization_barrier((later, left, part))
+    joined = call(join_kernel, shape((AUX, span * (n_col - 1)), BF16), early, *later)
     far = across(joined)
     left, part = call(
         functools.partial(buddy_kernel, sizes, tall),
-        (shape((rows, 4 * packed), BF16), shape((packed - dims, rows), F32)),
+        (shape((3 * packed, rows), BF16), shape((packed - dims, rows), F32)),
         block, mate, buddy, left, part,
-        scratch=[pltpu.VMEM((rows // 2, 4 * packed), BF16), pltpu.VMEM((packed - dims, rows // 2), F32)],
+        scratch=[pltpu.VMEM((3 * packed, rows // 2), BF16), pltpu.VMEM((packed - dims, rows // 2), F32)],
         **size(1, 2),
+    )
+    part = call(
+        functools.partial(near_kernel, sizes, tall),
+        shape((packed - dims, rows), F32), left, part, early, *later, **size(len(column)),
     )
     part = call(
         functools.partial(add_kernel, sizes, tall),
-        shape((packed - dims, rows), F32), left, part, *column, **size(len(column)),
-    )
-    rest = [*beside, *far[::-1]]
+        shape((packed - dims, rows), F32), left, part, *beside, **size(len(beside)),
+    )
     part = call(
         functools.partial(last_kernel, sizes, tall),
-        product, left, part, *rest,
-        scratch=[pltpu.VMEM((packed - dims, rows), F32)], **size(len(beside) + len(far) * (n_col - 1)),
+        product, left, part, *far[::-1],
+        scratch=[pltpu.VMEM((packed - dims, rows), F32)], **size(len(far) * (n_col - 1)),
     )
     chip = call(chip_kernel, product, part, to_mate(part))
     update, gram = call(update_kernel, (shape((kvec, 2 * local), F32), shape((kvec, 128), F32)), chip, odd_buddy(chip))

time: 41 us -> 37 us (0.902)
  waiting for transfers between devices: 14 us -> 10.2 us
  Pallas kernels: 10.4 us -> 9.78 us
    ppermute x3, waiting for transfers between devices: 3.17 us -> 1.19 us  [along(): lax.ppermute(x, 'col', list(enumerate(partners(n_col, step))))]
    ppermute x1, starting transfers between devices: 2.82 us -> 1.56 us  [to_buddy(): return lax.ppermute(x, 'row', [(i, i ^ 2) for i in range(n_row)])]
    ppermute x3, waiting for transfers between devices: 2.11 us -> 1.26 us  [to_mate(): return lax.ppermute(x, 'row', [(i, i ^ 1) for i in range(n_row)])]
    ppermute x3, starting transfers between devices: 4.39 us -> 5.23 us  [along(): lax.ppermute(x, 'col', list(enumerate(partners(n_col, step))))]
    ppermute x4, starting transfers between devices: 3.71 us -> 4.49 us  [odd_only(): return lax.ppermute(x, ('row', 'col'), pairs)]
    ppermute x4, waiting for transfers between devices: 6.37 us -> 5.58 us  [odd_only(): return lax.ppermute(x, ('row', 'col'), pairs)]
    pallas_call x11 -> x13, Pallas kernels: 10.4 us -> 9.78 us  [call(): pl.pallas_call(kernel, out_shape=jax.tree.map(lambda s: pltpu.VMEM(s.shap...]
  transfers between devices with their start and end apart: 15 -> 15, of which waited for: 10 -> 8; matrix products, arithmetic and copies ran while one was open for 0% -> 0% of each run, Pallas kernels for 10% -> 13%
where the time goes in v2:
time: 37 us; the launch traced here: 36.8 us
  starting transfers between devices  16.8 us (45%)
  waiting for transfers between devices  10.2 us (28%)
  Pallas kernels  9.78 us (26%)
    pallas_call x13, Pallas kernels, call(): pl.pallas_call(kernel, out_shape=jax.tree.map(lambda s: pltpu.VMEM(s.shap...  9.78 us
    ppermute x4, waiting for transfers between devices, odd_only(): return lax.ppermute(x, ('row', 'col'), pairs)  5.58 us
    ppermute x3, starting transfers between devices, along(): lax.ppermute(x, 'col', list(enumerate(partners(n_col, step))))  5.23 us
    ppermute x4, starting transfers between devices, odd_only(): return lax.ppermute(x, ('row', 'col'), pairs)  4.49 us
    ppermute x2, starting transfers between devices, across(): lax.ppermute(x, 'row', [(4 * i + k, 4 * j + k) for i, j in enumerate(part...  3.1 us
    ppermute x2, waiting for transfers between devices, odd_across(): lax.ppermute(x, 'row', [(i, place(i, step)) for i in range(n_row)])  2.12 us
    ppermute x2, starting transfers between devices, odd_across(): lax.ppermute(x, 'row', [(i, place(i, step)) for i in range(n_row)])  1.86 us
    ppermute x1, starting transfers between devices, to_buddy(): return lax.ppermute(x, 'row', [(i, i ^ 2) for i in range(n_row)])  1.56 us
  transfers between devices with their start and end apart: 15, of which 8 were waited for; matrix products, arithmetic and copies ran while one was open for 0% of the time, Pallas kernels for 13%

profile of v2, /device:TPU:0, one launch (start us, length us, event | category | flops | bytes accessed | tf_op | source)
XLA Modules:
  0.0 36.8 jit_solution(16875563221530777954)
XLA Ops:
  0.0 0.7 %shard_map.37.refs_0_.own_ref = bf16[8,1664]{1,0:T(8,128)(2,1)S(1)} custom-call(bf16[16,512]{1,0:T(8,128)(2,1)} %points_ref.1, bf16[512]{0:T(512)(128)(2,1)} %spread_ref.1, bf16[8,512]{1,0:T(8,128)(2,1)} %vectors_ref.1), custom_call_target="tpu_custom_call" | custom-call | flops 1000000 | bytes 100000 | tf_op jit(solution)/shard_map/pallas_call | solution.py:20
  0.7 0.6 %collective-permute-start = (bf16[8,1664]{1,0:T(8,128)(2,1)S(1)}, bf16[8,1664]{1,0:T(8,128)(2,1)S(1)}, u32[]{:S(2)}, u32[]{:S(2)}) collective-permute-start(bf16[8,1664]{1,0:T(8,128)(2,1)S(1)} %shard_map.37.refs_0_.own_ref), channel_id=1, source_target_pairs={{0,4},{4,0},{8,12},{12,8},{16,20},{20,16},{24,28},{28,24},{1,5},{5... | collective-permute-start | bytes 79880 | tf_op jit(solution)/shard_map/ppermute | solution.py:251
  1.3 2.6 %collective-permute-start.2 = (bf16[8,1664]{1,0:T(8,128)(2,1)S(1)}, bf16[8,1664]{1,0:T(8,128)(2,1)S(1)}, u32[]{:S(2)}, u32[]{:S(2)}) collective-permute-start(bf16[8,1664]{1,0:T(8,128)(2,1)S(1)} %shard_map.37.refs_0_.own_ref), channel_id=1, source_target_pairs={{0,1},{1,0},{2,3},{3,2},{4,5},{5,4},{6,7},{7,6},{8,9},{9,8},{10,11... | collective-permute-start | bytes 79880 | tf_op jit(solution)/shard_map/ppermute | solution.py:254
  3.9 2.5 %collective-permute-start.3 = (bf16[8,1664]{1,0:T(8,128)(2,1)S(1)}, bf16[8,1664]{1,0:T(8,128)(2,1)S(1)}, u32[]{:S(2)}, u32[]{:S(2)}) collective-permute-start(bf16[8,1664]{1,0:T(8,128)(2,1)S(1)} %shard_map.37.refs_0_.own_ref), channel_id=1, source_target_pairs={{0,3},{1,2},{2,1},{3,0},{4,7},{5,6},{6,5},{7,4},{8,11},{9,10},{10,... | collective-permute-start | bytes 79880 | tf_op jit(solution)/shard_map/ppermute | solution.py:254
  6.4 0.1 collective-permute-start.4
  6.5 1.5 %collective-permute-start.5 = (bf16[8,1664]{1,0:T(8,128)(2,1)S(1)}, bf16[8,1664]{1,0:T(8,128)(2,1)S(1)}, u32[]{:S(2)}, u32[]{:S(2)}) collective-permute-start(bf16[8,1664]{1,0:T(8,128)(2,1)S(1)} %shard_map.37.refs_0_.own_ref), channel_id=1, source_target_pairs={{0,16},{4,20},{8,24},{12,28},{16,0},{20,4},{24,8},{28,12},{1,17},{... | collective-permute-start | bytes 79880 | tf_op jit(solution)/shard_map/ppermute | solution.py:261
  8.1 1.6 %collective-permute-start.1 = (bf16[8,3328]{1,0:T(8,128)(2,1)S(1)}, bf16[8,3328]{1,0:T(8,128)(2,1)S(1)}, u32[]{:S(2)}, u32[]{:S(2)}) collective-permute-start(bf16[8,3328]{1,0:T(8,128)(2,1)S(1)} %shard_map.38), channel_id=1, source_target_pairs={{0,8},{4,12},{8,0},{12,4},{16,24},{20,28},{24,16},{28,20},{1,9},{5... | collective-permute-start | bytes 159752 | tf_op jit(solution)/shard_map/ppermute | solution.py:257
  9.6 0.6 %shard_map.39 = (bf16[96,1024]{1,0:T(8,128)(2,1)S(1)}, f32[16,1024]{1,0:T(8,128)S(1)}) custom-call(bf16[8,1664]{1,0:T(8,128)(2,1)S(1)} %shard_map.37.refs_0_.own_ref, bf16[8,1664]{1,0:T(8,128)(2,1)S(1)} %collective-permute-done.refs_1_.mate_ref), custom_call_target="tpu_custom_call" | custom-call | flops 335544320 | bytes 1000000 | tf_op jit(solution)/shard_map/pallas_call | solution.py:20
  10.3 1.2 %collective-permute-done.4.refs_0_.early_ref = bf16[8,1664]{1,0:T(8,128)(2,1)S(1)} collective-permute-done((bf16[8,1664]{1,0:T(8,128)(2,1)S(1)}, bf16[8,1664]{1,0:T(8,128)(2,1)S(1)}, u32[]{:S(2)}, u32[]{:S(2)}) %collective-permute-start.4) | collective-permute-done | bytes 26656 | tf_op jit(solution)/shard_map/ppermute | solution.py:254
  11.5 0.6 %shard_map.40.part_ref = f32[16,1024]{1,0:T(8,128)S(1)} custom-call(bf16[96,1024]{1,0:T(8,128)(2,1)S(1)} %get-tuple-element.19.left_ref.upper_ref, f32[16,1024]{1,0:T(8,128)S(1)} %get-tuple-element.18.part_ref, bf16[8,1664]{1,0:T(8,128)(2,1)S(1)} %collective-permute-done.4.refs_0_.early_ref), custom_call_target="tpu_custom_call" | custom-call | flops 335544320 | bytes 1000000 | tf_op jit(solution)/shard_map/pallas_call | solution.py:20
  12.1 0.0 collective-permute-done.2.refs_0_.refs_1_
  12.1 1.6 %collective-permute-start.6 = (bf16[8,4992]{1,0:T(8,128)(2,1)S(1)}, bf16[8,4992]{1,0:T(8,128)(2,1)S(1)}, u32[]{:S(2)}, u32[]{:S(2)}) collective-permute-start(bf16[8,4992]{1,0:T(8,128)(2,1)S(1)} %shard_map.44), channel_id=1, source_target_pairs={{0,16},{4,20},{8,24},{12,28},{16,0},{20,4},{24,8},{28,12},{1,17},{... | collective-permute-start | bytes 239624 | tf_op jit(solution)/shard_map/ppermute | solution.py:261
  13.7 0.1 shard_map.41
  13.8 2.4 %shard_map.42.part_ref = f32[16,2048]{1,0:T(8,128)S(1)} custom-call(bf16[96,2048]{1,0:T(8,128)(2,1)S(1)} %get-tuple-element.21.left_ref, f32[16,2048]{1,0:T(8,128)S(1)} %get-tuple-element.22.part_ref, bf16[8,1664]{1,0:T(8,128)(2,1)S(1)} %collective-permute-done.4.refs_0_.early_ref, bf16[8,1664]{1,0:T(8,128)(2,1)S(1)} %collective-permute-done.2.refs_0_.refs_1_, ...), custom_call_target="tpu_custom_call" | custom-call | flops 2013265920 | bytes 1000000 | tf_op jit(solution)/shard_map/pallas_call | solution.py:20
  16.2 1.1 %shard_map.43.part_ref = f32[16,2048]{1,0:T(8,128)S(1)} custom-call(bf16[96,2048]{1,0:T(8,128)(2,1)S(1)} %get-tuple-element.21.left_ref, f32[16,2048]{1,0:T(8,128)S(1)} %shard_map.42.part_ref, bf16[8,1664]{1,0:T(8,128)(2,1)S(1)} %collective-permute-done.5.refs_0_), custom_call_target="tpu_custom_call" | custom-call | flops 671088640 | bytes 1000000 | tf_op jit(solution)/shard_map/pallas_call | solution.py:20
  17.2 2.8 %shard_map.45.mine_ref = f32[8,2304]{1,0:T(8,128)S(1)} custom-call(bf16[96,2048]{1,0:T(8,128)(2,1)S(1)} %get-tuple-element.21.left_ref, f32[16,2048]{1,0:T(8,128)S(1)} %shard_map.43.part_ref, bf16[8,4992]{1,0:T(8,128)(2,1)S(1)} %collective-permute-done.6.refs_0_), custom_call_target="tpu_custom_call" | custom-call | flops 2013265920 | bytes 1000000 | tf_op jit(solution)/shard_map/pallas_call | solution.py:20
  20.0 0.0 collective-permute-start.7
  20.1 1.3 %collective-permute-done.7.other_ref = f32[8,2304]{1,0:T(8,128)S(1)} collective-permute-done((f32[8,2304]{1,0:T(8,128)S(1)}, f32[8,2304]{1,0:T(8,128)S(1)}, u32[]{:S(2)}, u32[]{:S(2)}) %collective-permute-start.7) | collective-permute-done | bytes 73760 | tf_op jit(solution)/shard_map/ppermute | solution.py:251
  21.4 0.9 %collective-permute-start.8 = (f32[8,2304]{1,0:T(8,128)S(1)}, f32[8,2304]{1,0:T(8,128)S(1)}, u32[]{:S(2)}, u32[]{:S(2)}) collective-permute-start(f32[8,2304]{1,0:T(8,128)S(1)} %shard_map.46.mine_ref), channel_id=1, source_target_pairs={{0,16},{1,17},{2,18},{3,19},{4,12},{5,13},{6,14},{7,15},{8,24},{9,... | collective-permute-start | bytes 221192 | tf_op jit(solution)/shard_map/ppermute | solution.py:272
  22.3 3.5 %collective-permute-done.8.other_ref = f32[8,2304]{1,0:T(8,128)S(1)} collective-permute-done((f32[8,2304]{1,0:T(8,128)S(1)}, f32[8,2304]{1,0:T(8,128)S(1)}, u32[]{:S(2)}, u32[]{:S(2)}) %collective-permute-start.8) | collective-permute-done | bytes 73760 | tf_op jit(solution)/shard_map/ppermute | solution.py:272
  25.8 0.1 shard_map.47
  25.9 1.5 %collective-permute-start.9 = (f32[8,128]{1,0:T(8,128)S(1)}, f32[8,128]{1,0:T(8,128)S(1)}, u32[]{:S(2)}, u32[]{:S(2)}) collective-permute-start(f32[8,128]{1,0:T(8,128)S(1)} %get-tuple-element.26.refs_0_), channel_id=1, source_target_pairs={{0,8},{1,9},{2,10},{3,11},{4,5},{5,4},{6,7},{7,6},{8,0},{9,1},{10,... | collective-permute-start | bytes 12296 | tf_op jit(solution)/shard_map/ppermute | solution.py:272
  27.4 0.5 %collective-permute-start.10 = (f32[8,128]{1,0:T(8,128)S(1)}, f32[8,128]{1,0:T(8,128)S(1)}, u32[]{:S(2)}, u32[]{:S(2)}) collective-permute-start(f32[8,128]{1,0:T(8,128)S(1)} %get-tuple-element.26.refs_0_), channel_id=1, source_target_pairs={{0,8},{1,9},{2,10},{3,11},{4,6},{5,7},{6,4},{7,5},{8,0},{9,1},{10,... | collective-permute-start | bytes 12296 | tf_op jit(solution)/shard_map/ppermute | solution.py:272
  28.0 1.5 %collective-permute-start.11 = (f32[8,128]{1,0:T(8,128)S(1)}, f32[8,128]{1,0:T(8,128)S(1)}, u32[]{:S(2)}, u32[]{:S(2)}) collective-permute-start(f32[8,128]{1,0:T(8,128)S(1)} %get-tuple-element.26.refs_0_), channel_id=1, source_target_pairs={{0,8},{1,9},{2,10},{3,11},{4,7},{5,6},{6,5},{7,4},{8,0},{9,1},{10,... | collective-permute-start | bytes 12296 | tf_op jit(solution)/shard_map/ppermute | solution.py:272
  29.5 0.1 collective-permute-done.9.refs_1_
  29.6 1.5 %collective-permute-done.10.refs_2_ = f32[8,128]{1,0:T(8,128)S(1)} collective-permute-done((f32[8,128]{1,0:T(8,128)S(1)}, f32[8,128]{1,0:T(8,128)S(1)}, u32[]{:S(2)}, u32[]{:S(2)}) %collective-permute-start.10) | collective-permute-done | bytes 4128 | tf_op jit(solution)/shard_map/ppermute | solution.py:272
  31.1 0.5 %collective-permute-done.11.refs_3_ = f32[8,128]{1,0:T(8,128)S(1)} collective-permute-done((f32[8,128]{1,0:T(8,128)S(1)}, f32[8,128]{1,0:T(8,128)S(1)}, u32[]{:S(2)}, u32[]{:S(2)}) %collective-permute-start.11) | collective-permute-done | bytes 4128 | tf_op jit(solution)/shard_map/ppermute | solution.py:272
  31.6 0.9 %collective-permute-start.13 = (f32[8,128]{1,0:T(8,128)S(1)}, f32[8,128]{1,0:T(8,128)S(1)}, u32[]{:S(2)}, u32[]{:S(2)}) collective-permute-start(f32[8,128]{1,0:T(8,128)S(1)} %get-tuple-element.27.line_ref), channel_id=1, source_target_pairs={{0,16},{4,20},{8,24},{12,28},{16,0},{20,4},{24,8},{28,12},{1,17},{... | collective-permute-start | bytes 12296 | tf_op jit(solution)/shard_map/ppermute | solution.py:280
  32.5 0.9 %collective-permute-start.14 = (f32[8,128]{1,0:T(8,128)S(1)}, f32[8,128]{1,0:T(8,128)S(1)}, u32[]{:S(2)}, u32[]{:S(2)}) collective-permute-start(f32[8,128]{1,0:T(8,128)S(1)} %get-tuple-element.27.line_ref), channel_id=1, source_target_pairs={{0,20},{4,16},{8,28},{12,24},{16,4},{20,0},{24,12},{28,8},{1,21},{... | collective-permute-start | bytes 12296 | tf_op jit(solution)/shard_map/ppermute | solution.py:280
  33.5 1.8 %collective-permute-done.13.refs_0_ = f32[8,128]{1,0:T(8,128)S(1)} collective-permute-done((f32[8,128]{1,0:T(8,128)S(1)}, f32[8,128]{1,0:T(8,128)S(1)}, u32[]{:S(2)}, u32[]{:S(2)}) %collective-permute-start.13) | collective-permute-done | bytes 4128 | tf_op jit(solution)/shard_map/ppermute | solution.py:280
  35.3 0.3 collective-permute-done.14.refs_1_
  35.6 1.3 %shard_map.49 = f32[8,512]{1,0:T(8,128)} custom-call(f32[8,1024]{1,0:T(8,128)S(1)} %get-tuple-element.25.update_ref, f32[8,128]{1,0:T(8,128)S(1)} %get-tuple-element.27.line_ref, f32[8,640]{1,0:T(8,128)S(1)} %collective-permute-done.12.given_ref, f32[8,128]{1,0:T(8,128)S(1)} %collective-permute-done.13.refs_0_, f32[8,128]{1,0:T(8,128)S(1)} %collective-permute-done.14.refs_1_), custom_call_target="tpu_custom_call" | custom-call | flops 1000000 | bytes 100000 | tf_op jit(solution)/shard_map/pallas_call | solution.py:20
  (11 shorter events, 0.1 us)
Async XLA Ops:
  0.7 7.3 %collective-permute-start = (bf16[8,1664]{1,0:T(8,128)(2,1)S(1)}, bf16[8,1664]{1,0:T(8,128)(2,1)S(1)}, u32[]{:S(2)}, u32[]{:S(2)}) collective-permute-start(bf16[8,1664]{1,0:T(8,128)(2,1)S(1)} %shard_map.37.refs_0_.own_ref), channel_id=1, source_target_pairs={{0,4},{4,0},{8,12},{12,8},{16,20},{20,16},{24,28},{28,24},{1,5},{5... | collective-permute-start | bytes 79880 | tf_op jit(solution)/shard_map/ppermute | solution.py:251
  1.3 10.8 %collective-permute-start.2 = (bf16[8,1664]{1,0:T(8,128)(2,1)S(1)}, bf16[8,1664]{1,0:T(8,128)(2,1)S(1)}, u32[]{:S(2)}, u32[]{:S(2)}) collective-permute-start(bf16[8,1664]{1,0:T(8,128)(2,1)S(1)} %shard_map.37.refs_0_.own_ref), channel_id=1, source_target_pairs={{0,1},{1,0},{2,3},{3,2},{4,5},{5,4},{6,7},{7,6},{8,9},{9,8},{10,11... | collective-permute-start | bytes 79880 | tf_op jit(solution)/shard_map/ppermute | solution.py:254
  3.9 8.2 %collective-permute-start.3 = (bf16[8,1664]{1,0:T(8,128)(2,1)S(1)}, bf16[8,1664]{1,0:T(8,128)(2,1)S(1)}, u32[]{:S(2)}, u32[]{:S(2)}) collective-permute-start(bf16[8,1664]{1,0:T(8,128)(2,1)S(1)} %shard_map.37.refs_0_.own_ref), channel_id=1, source_target_pairs={{0,3},{1,2},{2,1},{3,0},{4,7},{5,6},{6,5},{7,4},{8,11},{9,10},{10,... | collective-permute-start | bytes 79880 | tf_op jit(solution)/shard_map/ppermute | solution.py:254
  6.4 5.0 %collective-permute-start.4 = (bf16[8,1664]{1,0:T(8,128)(2,1)S(1)}, bf16[8,1664]{1,0:T(8,128)(2,1)S(1)}, u32[]{:S(2)}, u32[]{:S(2)}) collective-permute-start(bf16[8,1664]{1,0:T(8,128)(2,1)S(1)} %shard_map.37.refs_0_.own_ref), channel_id=1, source_target_pairs={{0,2},{1,3},{2,0},{3,1},{4,6},{5,7},{6,4},{7,5},{8,10},{9,11},{10,... | collective-permute-start | bytes 79880 | tf_op jit(solution)/shard_map/ppermute | solution.py:254
  6.5 9.6 %collective-permute-start.5 = (bf16[8,1664]{1,0:T(8,128)(2,1)S(1)}, bf16[8,1664]{1,0:T(8,128)(2,1)S(1)}, u32[]{:S(2)}, u32[]{:S(2)}) collective-permute-start(bf16[8,1664]{1,0:T(8,128)(2,1)S(1)} %shard_map.37.refs_0_.own_ref), channel_id=1, source_target_pairs={{0,16},{4,20},{8,24},{12,28},{16,0},{20,4},{24,8},{28,12},{1,17},{... | collective-permute-start | bytes 79880 | tf_op jit(solution)/shard_map/ppermute | solution.py:261
  8.1 5.6 %collective-permute-start.1 = (bf16[8,3328]{1,0:T(8,128)(2,1)S(1)}, bf16[8,3328]{1,0:T(8,128)(2,1)S(1)}, u32[]{:S(2)}, u32[]{:S(2)}) collective-permute-start(bf16[8,3328]{1,0:T(8,128)(2,1)S(1)} %shard_map.38), channel_id=1, source_target_pairs={{0,8},{4,12},{8,0},{12,4},{16,24},{20,28},{24,16},{28,20},{1,9},{5... | collective-permute-start | bytes 159752 | tf_op jit(solution)/shard_map/ppermute | solution.py:257
  12.1 5.1 %collective-permute-start.6 = (bf16[8,4992]{1,0:T(8,128)(2,1)S(1)}, bf16[8,4992]{1,0:T(8,128)(2,1)S(1)}, u32[]{:S(2)}, u32[]{:S(2)}) collective-permute-start(bf16[8,4992]{1,0:T(8,128)(2,1)S(1)} %shard_map.44), channel_id=1, source_target_pairs={{0,16},{4,20},{8,24},{12,28},{16,0},{20,4},{24,8},{28,12},{1,17},{... | collective-permute-start | bytes 239624 | tf_op jit(solution)/shard_map/ppermute | solution.py:261
  20.0 1.3 %collective-permute-start.7 = (f32[8,2304]{1,0:T(8,128)S(1)}, f32[8,2304]{1,0:T(8,128)S(1)}, u32[]{:S(2)}, u32[]{:S(2)}) collective-permute-start(f32[8,2304]{1,0:T(8,128)S(1)} %shard_map.45.mine_ref), channel_id=1, source_target_pairs={{0,4},{4,0},{8,12},{12,8},{16,20},{20,16},{24,28},{28,24},{1,5},{5... | collective-permute-start | bytes 221192 | tf_op jit(solution)/shard_map/ppermute | solution.py:251
  21.4 4.4 %collective-permute-start.8 = (f32[8,2304]{1,0:T(8,128)S(1)}, f32[8,2304]{1,0:T(8,128)S(1)}, u32[]{:S(2)}, u32[]{:S(2)}) collective-permute-start(f32[8,2304]{1,0:T(8,128)S(1)} %shard_map.46.mine_ref), channel_id=1, source_target_pairs={{0,16},{1,17},{2,18},{3,19},{4,12},{5,13},{6,14},{7,15},{8,24},{9,... | collective-permute-start | bytes 221192 | tf_op jit(solution)/shard_map/ppermute | solution.py:272
  25.9 3.6 %collective-permute-start.9 = (f32[8,128]{1,0:T(8,128)S(1)}, f32[8,128]{1,0:T(8,128)S(1)}, u32[]{:S(2)}, u32[]{:S(2)}) collective-permute-start(f32[8,128]{1,0:T(8,128)S(1)} %get-tuple-element.26.refs_0_), channel_id=1, source_target_pairs={{0,8},{1,9},{2,10},{3,11},{4,5},{5,4},{6,7},{7,6},{8,0},{9,1},{10,... | collective-permute-start | bytes 12296 | tf_op jit(solution)/shard_map/ppermute | solution.py:272
  27.4 3.6 %collective-permute-start.10 = (f32[8,128]{1,0:T(8,128)S(1)}, f32[8,128]{1,0:T(8,128)S(1)}, u32[]{:S(2)}, u32[]{:S(2)}) collective-permute-start(f32[8,128]{1,0:T(8,128)S(1)} %get-tuple-element.26.refs_0_), channel_id=1, source_target_pairs={{0,8},{1,9},{2,10},{3,11},{4,6},{5,7},{6,4},{7,5},{8,0},{9,1},{10,... | collective-permute-start | bytes 12296 | tf_op jit(solution)/shard_map/ppermute | solution.py:272
  28.0 3.6 %collective-permute-start.11 = (f32[8,128]{1,0:T(8,128)S(1)}, f32[8,128]{1,0:T(8,128)S(1)}, u32[]{:S(2)}, u32[]{:S(2)}) collective-permute-start(f32[8,128]{1,0:T(8,128)S(1)} %get-tuple-element.26.refs_0_), channel_id=1, source_target_pairs={{0,8},{1,9},{2,10},{3,11},{4,7},{5,6},{6,5},{7,4},{8,0},{9,1},{10,... | collective-permute-start | bytes 12296 | tf_op jit(solution)/shard_map/ppermute | solution.py:272
  31.6 4.0 %collective-permute-start.12 = (f32[8,640]{1,0:T(8,128)S(1)}, f32[8,640]{1,0:T(8,128)S(1)}, u32[]{:S(2)}, u32[]{:S(2)}) collective-permute-start(f32[8,640]{1,0:T(8,128)S(1)} %get-tuple-element.28), channel_id=1, source_target_pairs={{0,4},{4,0},{8,12},{12,8},{16,20},{20,16},{24,28},{28,24},{1,5},{5... | collective-permute-start | bytes 61448 | tf_op jit(solution)/shard_map/ppermute | solution.py:251
  31.6 3.7 %collective-permute-start.13 = (f32[8,128]{1,0:T(8,128)S(1)}, f32[8,128]{1,0:T(8,128)S(1)}, u32[]{:S(2)}, u32[]{:S(2)}) collective-permute-start(f32[8,128]{1,0:T(8,128)S(1)} %get-tuple-element.27.line_ref), channel_id=1, source_target_pairs={{0,16},{4,20},{8,24},{12,28},{16,0},{20,4},{24,8},{28,12},{1,17},{... | collective-permute-start | bytes 12296 | tf_op jit(solution)/shard_map/ppermute | solution.py:280
  32.5 3.0 %collective-permute-start.14 = (f32[8,128]{1,0:T(8,128)S(1)}, f32[8,128]{1,0:T(8,128)S(1)}, u32[]{:S(2)}, u32[]{:S(2)}) collective-permute-start(f32[8,128]{1,0:T(8,128)S(1)} %get-tuple-element.27.line_ref), channel_id=1, source_target_pairs={{0,20},{4,16},{8,28},{12,24},{16,4},{20,0},{24,12},{28,8},{1,21},{... | collective-permute-start | bytes 12296 | tf_op jit(solution)/shard_map/ppermute | solution.py:280

commit v3 on v2

--- a/solution.py
+++ b/solution.py
@@ -224,13 +224,16 @@
     rest = jnp.where(odd, update_ref[:, :local], given_ref[:, :local])
     kvec = rest.shape[0]
     row = lax.broadcasted_iota(jnp.int32, gram.shape, 0)
-    column = lax.broadcasted_iota(jnp.int32, gram.shape, 1)
-    for k in range(kvec - 1):
-        factor = jnp.where(row[:, :1] > k, gram[:, k : k + 1] / gram[k : k + 1, k : k + 1], F32(0))
-        rest = rest - factor * rest[k : k + 1]
-        gram = gram - factor * gram[k : k + 1]
-    pivot = jnp.sum(jnp.where(row == column, gram, F32(0)), axis=1, keepdims=True)
-    out_ref[...] = rest * (root / jnp.sqrt(pivot))
+    spread_out = lambda x: jnp.concatenate([x] * (local // 128), axis=1)
+    columns = [jnp.broadcast_to(gram[:, k : k + 1], gram.shape) for k in range(kvec)]
+    pivot = columns[0]
+    for k in range(kvec):
+        pivot = jnp.where(row == k, columns[k], pivot)
+        factor = jnp.where(row > k, columns[k] / columns[k][k : k + 1], F32(0))
+        for j in range(k + 1, kvec):
+            columns[j] = columns[j] - factor * columns[j][k : k + 1]
+        rest = rest - spread_out(factor) * rest[k : k + 1]
+    out_ref[...] = rest * spread_out(root / jnp.sqrt(pivot))
 
 
 def partners(count, step):
@@ -280,7 +283,7 @@
         return [lax.ppermute(x, "row", [(i, place(i, step)) for i in range(n_row)]) for step in others]
 
     def odd_buddy(x):
-        return odd_only(x, lambda i, j: (i ^ 2, j), 4 if n_row % 8 == 0 else 2)
+        return odd_only(x, lambda i, j: (i ^ 2, j), 2)
 
     shape = jax.ShapeDtypeStruct
     block = call(pack_kernel, shape((AUX, span), BF16), points, spread, vectors, in_hbm=True)

time: 37 us -> 36.5 us (0.986)
  starting transfers between devices: 16.8 us -> 17.5 us
  waiting for transfers between devices: 10.2 us -> 9.54 us
  Pallas kernels: 9.78 us -> 9.33 us
    ppermute x4, waiting for transfers between devices: 5.58 us -> 4.96 us  [odd_only(): return lax.ppermute(x, ('row', 'col'), pairs)]
    ppermute x4, starting transfers between devices: 4.49 us -> 5.11 us  [odd_only(): return lax.ppermute(x, ('row', 'col'), pairs)]
    pallas_call x13, Pallas kernels: 9.78 us -> 9.33 us  [call(): pl.pallas_call(kernel, out_shape=jax.tree.map(lambda s: pltpu.VMEM(s.shap...]
where the time goes in v3:
time: 36.5 us; the launch traced here: 36.4 us
  starting transfers between devices  17.5 us (48%)
  waiting for transfers between devices  9.54 us (26%)
  Pallas kernels  9.33 us (26%)
    pallas_call x13, Pallas kernels, call(): pl.pallas_call(kernel, out_shape=jax.tree.map(lambda s: pltpu.VMEM(s.shap...  9.33 us
    ppermute x3, starting transfers between devices, along(): lax.ppermute(x, 'col', list(enumerate(partners(n_col, step))))  5.23 us
    ppermute x4, starting transfers between devices, odd_only(): return lax.ppermute(x, ('row', 'col'), pairs)  5.11 us
    ppermute x4, waiting for transfers between devices, odd_only(): return lax.ppermute(x, ('row', 'col'), pairs)  4.96 us
    ppermute x2, starting transfers between devices, across(): lax.ppermute(x, 'row', [(4 * i + k, 4 * j + k) for i, j in enumerate(part...  3.1 us
    ppermute x2, waiting for transfers between devices, odd_across(): lax.ppermute(x, 'row', [(i, place(i, step)) for i in range(n_row)])  2.12 us
    ppermute x2, starting transfers between devices, odd_across(): lax.ppermute(x, 'row', [(i, place(i, step)) for i in range(n_row)])  1.77 us
    ppermute x1, starting transfers between devices, to_buddy(): return lax.ppermute(x, 'row', [(i, i ^ 2) for i in range(n_row)])  1.56 us
  transfers between devices with their start and end apart: 15, of which 8 were waited for; matrix products, arithmetic and copies ran while one was open for 0% of the time, Pallas kernels for 13%

profile of v3, /device:TPU:0, one launch (start us, length us, event | category | flops | bytes accessed | tf_op | source)
XLA Modules:
  0.0 36.4 jit_solution(5259186049394526555)
XLA Ops:
  0.0 0.7 %shard_map.37.refs_0_.own_ref = bf16[8,1664]{1,0:T(8,128)(2,1)S(1)} custom-call(bf16[16,512]{1,0:T(8,128)(2,1)} %points_ref.1, bf16[512]{0:T(512)(128)(2,1)} %spread_ref.1, bf16[8,512]{1,0:T(8,128)(2,1)} %vectors_ref.1), custom_call_target="tpu_custom_call" | custom-call | flops 1000000 | bytes 100000 | tf_op jit(solution)/shard_map/pallas_call | solution.py:20
  0.7 0.6 %collective-permute-start = (bf16[8,1664]{1,0:T(8,128)(2,1)S(1)}, bf16[8,1664]{1,0:T(8,128)(2,1)S(1)}, u32[]{:S(2)}, u32[]{:S(2)}) collective-permute-start(bf16[8,1664]{1,0:T(8,128)(2,1)S(1)} %shard_map.37.refs_0_.own_ref), channel_id=1, source_target_pairs={{0,4},{4,0},{8,12},{12,8},{16,20},{20,16},{24,28},{28,24},{1,5},{5... | collective-permute-start | bytes 79880 | tf_op jit(solution)/shard_map/ppermute | solution.py:254
  1.3 2.6 %collective-permute-start.2 = (bf16[8,1664]{1,0:T(8,128)(2,1)S(1)}, bf16[8,1664]{1,0:T(8,128)(2,1)S(1)}, u32[]{:S(2)}, u32[]{:S(2)}) collective-permute-start(bf16[8,1664]{1,0:T(8,128)(2,1)S(1)} %shard_map.37.refs_0_.own_ref), channel_id=1, source_target_pairs={{0,1},{1,0},{2,3},{3,2},{4,5},{5,4},{6,7},{7,6},{8,9},{9,8},{10,11... | collective-permute-start | bytes 79880 | tf_op jit(solution)/shard_map/ppermute | solution.py:257
  3.9 2.5 %collective-permute-start.3 = (bf16[8,1664]{1,0:T(8,128)(2,1)S(1)}, bf16[8,1664]{1,0:T(8,128)(2,1)S(1)}, u32[]{:S(2)}, u32[]{:S(2)}) collective-permute-start(bf16[8,1664]{1,0:T(8,128)(2,1)S(1)} %shard_map.37.refs_0_.own_ref), channel_id=1, source_target_pairs={{0,3},{1,2},{2,1},{3,0},{4,7},{5,6},{6,5},{7,4},{8,11},{9,10},{10,... | collective-permute-start | bytes 79880 | tf_op jit(solution)/shard_map/ppermute | solution.py:257
  6.4 0.1 collective-permute-start.4
  6.5 1.5 %collective-permute-start.5 = (bf16[8,1664]{1,0:T(8,128)(2,1)S(1)}, bf16[8,1664]{1,0:T(8,128)(2,1)S(1)}, u32[]{:S(2)}, u32[]{:S(2)}) collective-permute-start(bf16[8,1664]{1,0:T(8,128)(2,1)S(1)} %shard_map.37.refs_0_.own_ref), channel_id=1, source_target_pairs={{0,16},{4,20},{8,24},{12,28},{16,0},{20,4},{24,8},{28,12},{1,17},{... | collective-permute-start | bytes 79880 | tf_op jit(solution)/shard_map/ppermute | solution.py:264
  8.1 1.6 %collective-permute-start.1 = (bf16[8,3328]{1,0:T(8,128)(2,1)S(1)}, bf16[8,3328]{1,0:T(8,128)(2,1)S(1)}, u32[]{:S(2)}, u32[]{:S(2)}) collective-permute-start(bf16[8,3328]{1,0:T(8,128)(2,1)S(1)} %shard_map.38), channel_id=1, source_target_pairs={{0,8},{4,12},{8,0},{12,4},{16,24},{20,28},{24,16},{28,20},{1,9},{5... | collective-permute-start | bytes 159752 | tf_op jit(solution)/shard_map/ppermute | solution.py:260
  9.6 0.6 %shard_map.39 = (bf16[96,1024]{1,0:T(8,128)(2,1)S(1)}, f32[16,1024]{1,0:T(8,128)S(1)}) custom-call(bf16[8,1664]{1,0:T(8,128)(2,1)S(1)} %shard_map.37.refs_0_.own_ref, bf16[8,1664]{1,0:T(8,128)(2,1)S(1)} %collective-permute-done.refs_1_.mate_ref), custom_call_target="tpu_custom_call" | custom-call | flops 335544320 | bytes 1000000 | tf_op jit(solution)/shard_map/pallas_call | solution.py:20
  10.3 1.2 %collective-permute-done.4.refs_0_.early_ref = bf16[8,1664]{1,0:T(8,128)(2,1)S(1)} collective-permute-done((bf16[8,1664]{1,0:T(8,128)(2,1)S(1)}, bf16[8,1664]{1,0:T(8,128)(2,1)S(1)}, u32[]{:S(2)}, u32[]{:S(2)}) %collective-permute-start.4) | collective-permute-done | bytes 26656 | tf_op jit(solution)/shard_map/ppermute | solution.py:257
  11.5 0.6 %shard_map.40.part_ref = f32[16,1024]{1,0:T(8,128)S(1)} custom-call(bf16[96,1024]{1,0:T(8,128)(2,1)S(1)} %get-tuple-element.19.left_ref.upper_ref, f32[16,1024]{1,0:T(8,128)S(1)} %get-tuple-element.18.part_ref, bf16[8,1664]{1,0:T(8,128)(2,1)S(1)} %collective-permute-done.4.refs_0_.early_ref), custom_call_target="tpu_custom_call" | custom-call | flops 335544320 | bytes 1000000 | tf_op jit(solution)/shard_map/pallas_call | solution.py:20
  12.1 1.6 %collective-permute-start.6 = (bf16[8,4992]{1,0:T(8,128)(2,1)S(1)}, bf16[8,4992]{1,0:T(8,128)(2,1)S(1)}, u32[]{:S(2)}, u32[]{:S(2)}) collective-permute-start(bf16[8,4992]{1,0:T(8,128)(2,1)S(1)} %shard_map.44), channel_id=1, source_target_pairs={{0,16},{4,20},{8,24},{12,28},{16,0},{20,4},{24,8},{28,12},{1,17},{... | collective-permute-start | bytes 239624 | tf_op jit(solution)/shard_map/ppermute | solution.py:264
  13.7 0.1 shard_map.41
  13.8 2.4 %shard_map.42.part_ref = f32[16,2048]{1,0:T(8,128)S(1)} custom-call(bf16[96,2048]{1,0:T(8,128)(2,1)S(1)} %get-tuple-element.21.left_ref, f32[16,2048]{1,0:T(8,128)S(1)} %get-tuple-element.22.part_ref, bf16[8,1664]{1,0:T(8,128)(2,1)S(1)} %collective-permute-done.4.refs_0_.early_ref, bf16[8,1664]{1,0:T(8,128)(2,1)S(1)} %collective-permute-done.2.refs_0_.refs_1_, ...), custom_call_target="tpu_custom_call" | custom-call | flops 2013265920 | bytes 1000000 | tf_op jit(solution)/shard_map/pallas_call | solution.py:20
  16.2 1.1 %shard_map.43.part_ref = f32[16,2048]{1,0:T(8,128)S(1)} custom-call(bf16[96,2048]{1,0:T(8,128)(2,1)S(1)} %get-tuple-element.21.left_ref, f32[16,2048]{1,0:T(8,128)S(1)} %shard_map.42.part_ref, bf16[8,1664]{1,0:T(8,128)(2,1)S(1)} %collective-permute-done.5.refs_0_), custom_call_target="tpu_custom_call" | custom-call | flops 671088640 | bytes 1000000 | tf_op jit(solution)/shard_map/pallas_call | solution.py:20
  17.2 2.8 %shard_map.45.mine_ref = f32[8,2304]{1,0:T(8,128)S(1)} custom-call(bf16[96,2048]{1,0:T(8,128)(2,1)S(1)} %get-tuple-element.21.left_ref, f32[16,2048]{1,0:T(8,128)S(1)} %shard_map.43.part_ref, bf16[8,4992]{1,0:T(8,128)(2,1)S(1)} %collective-permute-done.6.refs_0_), custom_call_target="tpu_custom_call" | custom-call | flops 2013265920 | bytes 1000000 | tf_op jit(solution)/shard_map/pallas_call | solution.py:20
  20.0 0.0 collective-permute-start.7
  20.1 1.3 %collective-permute-done.7.other_ref = f32[8,2304]{1,0:T(8,128)S(1)} collective-permute-done((f32[8,2304]{1,0:T(8,128)S(1)}, f32[8,2304]{1,0:T(8,128)S(1)}, u32[]{:S(2)}, u32[]{:S(2)}) %collective-permute-start.7) | collective-permute-done | bytes 73760 | tf_op jit(solution)/shard_map/ppermute | solution.py:254
  21.4 1.6 %collective-permute-start.8 = (f32[8,2304]{1,0:T(8,128)S(1)}, f32[8,2304]{1,0:T(8,128)S(1)}, u32[]{:S(2)}, u32[]{:S(2)}) collective-permute-start(f32[8,2304]{1,0:T(8,128)S(1)} %shard_map.46.mine_ref), channel_id=1, source_target_pairs={{0,8},{1,9},{2,10},{3,11},{4,12},{5,13},{6,14},{7,15},{8,0},{9,1},... | collective-permute-start | bytes 221192 | tf_op jit(solution)/shard_map/ppermute | solution.py:275
  22.9 2.9 %collective-permute-done.8.other_ref = f32[8,2304]{1,0:T(8,128)S(1)} collective-permute-done((f32[8,2304]{1,0:T(8,128)S(1)}, f32[8,2304]{1,0:T(8,128)S(1)}, u32[]{:S(2)}, u32[]{:S(2)}) %collective-permute-start.8) | collective-permute-done | bytes 73760 | tf_op jit(solution)/shard_map/ppermute | solution.py:275
  25.8 0.1 shard_map.47
  25.9 1.5 %collective-permute-start.9 = (f32[8,128]{1,0:T(8,128)S(1)}, f32[8,128]{1,0:T(8,128)S(1)}, u32[]{:S(2)}, u32[]{:S(2)}) collective-permute-start(f32[8,128]{1,0:T(8,128)S(1)} %get-tuple-element.26.refs_0_), channel_id=1, source_target_pairs={{0,8},{1,9},{2,10},{3,11},{4,5},{5,4},{6,7},{7,6},{8,0},{9,1},{10,... | collective-permute-start | bytes 12296 | tf_op jit(solution)/shard_map/ppermute | solution.py:275
  27.4 0.5 %collective-permute-start.10 = (f32[8,128]{1,0:T(8,128)S(1)}, f32[8,128]{1,0:T(8,128)S(1)}, u32[]{:S(2)}, u32[]{:S(2)}) collective-permute-start(f32[8,128]{1,0:T(8,128)S(1)} %get-tuple-element.26.refs_0_), channel_id=1, source_target_pairs={{0,8},{1,9},{2,10},{3,11},{4,6},{5,7},{6,4},{7,5},{8,0},{9,1},{10,... | collective-permute-start | bytes 12296 | tf_op jit(solution)/shard_map/ppermute | solution.py:275
  28.0 1.5 %collective-permute-start.11 = (f32[8,128]{1,0:T(8,128)S(1)}, f32[8,128]{1,0:T(8,128)S(1)}, u32[]{:S(2)}, u32[]{:S(2)}) collective-permute-start(f32[8,128]{1,0:T(8,128)S(1)} %get-tuple-element.26.refs_0_), channel_id=1, source_target_pairs={{0,8},{1,9},{2,10},{3,11},{4,7},{5,6},{6,5},{7,4},{8,0},{9,1},{10,... | collective-permute-start | bytes 12296 | tf_op jit(solution)/shard_map/ppermute | solution.py:275
  29.5 0.1 collective-permute-done.9.refs_1_
  29.6 1.5 %collective-permute-done.10.refs_2_ = f32[8,128]{1,0:T(8,128)S(1)} collective-permute-done((f32[8,128]{1,0:T(8,128)S(1)}, f32[8,128]{1,0:T(8,128)S(1)}, u32[]{:S(2)}, u32[]{:S(2)}) %collective-permute-start.10) | collective-permute-done | bytes 4128 | tf_op jit(solution)/shard_map/ppermute | solution.py:275
  31.1 0.5 %collective-permute-done.11.refs_3_ = f32[8,128]{1,0:T(8,128)S(1)} collective-permute-done((f32[8,128]{1,0:T(8,128)S(1)}, f32[8,128]{1,0:T(8,128)S(1)}, u32[]{:S(2)}, u32[]{:S(2)}) %collective-permute-start.11) | collective-permute-done | bytes 4128 | tf_op jit(solution)/shard_map/ppermute | solution.py:275
  31.6 0.1 collective-permute-start.12
  31.7 0.9 %collective-permute-start.13 = (f32[8,128]{1,0:T(8,128)S(1)}, f32[8,128]{1,0:T(8,128)S(1)}, u32[]{:S(2)}, u32[]{:S(2)}) collective-permute-start(f32[8,128]{1,0:T(8,128)S(1)} %get-tuple-element.27.line_ref), channel_id=1, source_target_pairs={{0,16},{4,20},{8,24},{12,28},{16,0},{20,4},{24,8},{28,12},{1,17},{... | collective-permute-start | bytes 12296 | tf_op jit(solution)/shard_map/ppermute | solution.py:283
  32.5 0.9 %collective-permute-start.14 = (f32[8,128]{1,0:T(8,128)S(1)}, f32[8,128]{1,0:T(8,128)S(1)}, u32[]{:S(2)}, u32[]{:S(2)}) collective-permute-start(f32[8,128]{1,0:T(8,128)S(1)} %get-tuple-element.27.line_ref), channel_id=1, source_target_pairs={{0,20},{4,16},{8,28},{12,24},{16,4},{20,0},{24,12},{28,8},{1,21},{... | collective-permute-start | bytes 12296 | tf_op jit(solution)/shard_map/ppermute | solution.py:283
  33.5 1.8 %collective-permute-done.13.refs_0_ = f32[8,128]{1,0:T(8,128)S(1)} collective-permute-done((f32[8,128]{1,0:T(8,128)S(1)}, f32[8,128]{1,0:T(8,128)S(1)}, u32[]{:S(2)}, u32[]{:S(2)}) %collective-permute-start.13) | collective-permute-done | bytes 4128 | tf_op jit(solution)/shard_map/ppermute | solution.py:283
  35.3 0.3 collective-permute-done.14.refs_1_
  35.6 0.8 %shard_map.49 = f32[8,512]{1,0:T(8,128)} custom-call(f32[8,1024]{1,0:T(8,128)S(1)} %get-tuple-element.25.update_ref, f32[8,128]{1,0:T(8,128)S(1)} %get-tuple-element.27.line_ref, f32[8,640]{1,0:T(8,128)S(1)} %collective-permute-done.12.given_ref, f32[8,128]{1,0:T(8,128)S(1)} %collective-permute-done.13.refs_0_, f32[8,128]{1,0:T(8,128)S(1)} %collective-permute-done.14.refs_1_), custom_call_target="tpu_custom_call" | custom-call | flops 1000000 | bytes 100000 | tf_op jit(solution)/shard_map/pallas_call | solution.py:20
  (11 shorter events, 0.1 us)
Async XLA Ops:
  0.7 7.3 %collective-permute-start = (bf16[8,1664]{1,0:T(8,128)(2,1)S(1)}, bf16[8,1664]{1,0:T(8,128)(2,1)S(1)}, u32[]{:S(2)}, u32[]{:S(2)}) collective-permute-start(bf16[8,1664]{1,0:T(8,128)(2,1)S(1)} %shard_map.37.refs_0_.own_ref), channel_id=1, source_target_pairs={{0,4},{4,0},{8,12},{12,8},{16,20},{20,16},{24,28},{28,24},{1,5},{5... | collective-permute-start | bytes 79880 | tf_op jit(solution)/shard_map/ppermute | solution.py:254
  1.3 10.8 %collective-permute-start.2 = (bf16[8,1664]{1,0:T(8,128)(2,1)S(1)}, bf16[8,1664]{1,0:T(8,128)(2,1)S(1)}, u32[]{:S(2)}, u32[]{:S(2)}) collective-permute-start(bf16[8,1664]{1,0:T(8,128)(2,1)S(1)} %shard_map.37.refs_0_.own_ref), channel_id=1, source_target_pairs={{0,1},{1,0},{2,3},{3,2},{4,5},{5,4},{6,7},{7,6},{8,9},{9,8},{10,11... | collective-permute-start | bytes 79880 | tf_op jit(solution)/shard_map/ppermute | solution.py:257
  3.9 8.2 %collective-permute-start.3 = (bf16[8,1664]{1,0:T(8,128)(2,1)S(1)}, bf16[8,1664]{1,0:T(8,128)(2,1)S(1)}, u32[]{:S(2)}, u32[]{:S(2)}) collective-permute-start(bf16[8,1664]{1,0:T(8,128)(2,1)S(1)} %shard_map.37.refs_0_.own_ref), channel_id=1, source_target_pairs={{0,3},{1,2},{2,1},{3,0},{4,7},{5,6},{6,5},{7,4},{8,11},{9,10},{10,... | collective-permute-start | bytes 79880 | tf_op jit(solution)/shard_map/ppermute | solution.py:257
  6.4 5.0 %collective-permute-start.4 = (bf16[8,1664]{1,0:T(8,128)(2,1)S(1)}, bf16[8,1664]{1,0:T(8,128)(2,1)S(1)}, u32[]{:S(2)}, u32[]{:S(2)}) collective-permute-start(bf16[8,1664]{1,0:T(8,128)(2,1)S(1)} %shard_map.37.refs_0_.own_ref), channel_id=1, source_target_pairs={{0,2},{1,3},{2,0},{3,1},{4,6},{5,7},{6,4},{7,5},{8,10},{9,11},{10,... | collective-permute-start | bytes 79880 | tf_op jit(solution)/shard_map/ppermute | solution.py:257
  6.5 9.6 %collective-permute-start.5 = (bf16[8,1664]{1,0:T(8,128)(2,1)S(1)}, bf16[8,1664]{1,0:T(8,128)(2,1)S(1)}, u32[]{:S(2)}, u32[]{:S(2)}) collective-permute-start(bf16[8,1664]{1,0:T(8,128)(2,1)S(1)} %shard_map.37.refs_0_.own_ref), channel_id=1, source_target_pairs={{0,16},{4,20},{8,24},{12,28},{16,0},{20,4},{24,8},{28,12},{1,17},{... | collective-permute-start | bytes 79880 | tf_op jit(solution)/shard_map/ppermute | solution.py:264
  8.1 5.6 %collective-permute-start.1 = (bf16[8,3328]{1,0:T(8,128)(2,1)S(1)}, bf16[8,3328]{1,0:T(8,128)(2,1)S(1)}, u32[]{:S(2)}, u32[]{:S(2)}) collective-permute-start(bf16[8,3328]{1,0:T(8,128)(2,1)S(1)} %shard_map.38), channel_id=1, source_target_pairs={{0,8},{4,12},{8,0},{12,4},{16,24},{20,28},{24,16},{28,20},{1,9},{5... | collective-permute-start | bytes 159752 | tf_op jit(solution)/shard_map/ppermute | solution.py:260
  12.1 5.1 %collective-permute-start.6 = (bf16[8,4992]{1,0:T(8,128)(2,1)S(1)}, bf16[8,4992]{1,0:T(8,128)(2,1)S(1)}, u32[]{:S(2)}, u32[]{:S(2)}) collective-permute-start(bf16[8,4992]{1,0:T(8,128)(2,1)S(1)} %shard_map.44), channel_id=1, source_target_pairs={{0,16},{4,20},{8,24},{12,28},{16,0},{20,4},{24,8},{28,12},{1,17},{... | collective-permute-start | bytes 239624 | tf_op jit(solution)/shard_map/ppermute | solution.py:264
  20.0 1.3 %collective-permute-start.7 = (f32[8,2304]{1,0:T(8,128)S(1)}, f32[8,2304]{1,0:T(8,128)S(1)}, u32[]{:S(2)}, u32[]{:S(2)}) collective-permute-start(f32[8,2304]{1,0:T(8,128)S(1)} %shard_map.45.mine_ref), channel_id=1, source_target_pairs={{0,4},{4,0},{8,12},{12,8},{16,20},{20,16},{24,28},{28,24},{1,5},{5... | collective-permute-start | bytes 221192 | tf_op jit(solution)/shard_map/ppermute | solution.py:254
  21.4 4.4 %collective-permute-start.8 = (f32[8,2304]{1,0:T(8,128)S(1)}, f32[8,2304]{1,0:T(8,128)S(1)}, u32[]{:S(2)}, u32[]{:S(2)}) collective-permute-start(f32[8,2304]{1,0:T(8,128)S(1)} %shard_map.46.mine_ref), channel_id=1, source_target_pairs={{0,8},{1,9},{2,10},{3,11},{4,12},{5,13},{6,14},{7,15},{8,0},{9,1},... | collective-permute-start | bytes 221192 | tf_op jit(solution)/shard_map/ppermute | solution.py:275
  25.9 3.6 %collective-permute-start.9 = (f32[8,128]{1,0:T(8,128)S(1)}, f32[8,128]{1,0:T(8,128)S(1)}, u32[]{:S(2)}, u32[]{:S(2)}) collective-permute-start(f32[8,128]{1,0:T(8,128)S(1)} %get-tuple-element.26.refs_0_), channel_id=1, source_target_pairs={{0,8},{1,9},{2,10},{3,11},{4,5},{5,4},{6,7},{7,6},{8,0},{9,1},{10,... | collective-permute-start | bytes 12296 | tf_op jit(solution)/shard_map/ppermute | solution.py:275
  27.4 3.6 %collective-permute-start.10 = (f32[8,128]{1,0:T(8,128)S(1)}, f32[8,128]{1,0:T(8,128)S(1)}, u32[]{:S(2)}, u32[]{:S(2)}) collective-permute-start(f32[8,128]{1,0:T(8,128)S(1)} %get-tuple-element.26.refs_0_), channel_id=1, source_target_pairs={{0,8},{1,9},{2,10},{3,11},{4,6},{5,7},{6,4},{7,5},{8,0},{9,1},{10,... | collective-permute-start | bytes 12296 | tf_op jit(solution)/shard_map/ppermute | solution.py:275
  28.0 3.6 %collective-permute-start.11 = (f32[8,128]{1,0:T(8,128)S(1)}, f32[8,128]{1,0:T(8,128)S(1)}, u32[]{:S(2)}, u32[]{:S(2)}) collective-permute-start(f32[8,128]{1,0:T(8,128)S(1)} %get-tuple-element.26.refs_0_), channel_id=1, source_target_pairs={{0,8},{1,9},{2,10},{3,11},{4,7},{5,6},{6,5},{7,4},{8,0},{9,1},{10,... | collective-permute-start | bytes 12296 | tf_op jit(solution)/shard_map/ppermute | solution.py:275
  31.6 4.0 %collective-permute-start.12 = (f32[8,640]{1,0:T(8,128)S(1)}, f32[8,640]{1,0:T(8,128)S(1)}, u32[]{:S(2)}, u32[]{:S(2)}) collective-permute-start(f32[8,640]{1,0:T(8,128)S(1)} %get-tuple-element.28), channel_id=1, source_target_pairs={{0,4},{4,0},{8,12},{12,8},{16,20},{20,16},{24,28},{28,24},{1,5},{5... | collective-permute-start | bytes 61448 | tf_op jit(solution)/shard_map/ppermute | solution.py:254
  31.7 3.6 %collective-permute-start.13 = (f32[8,128]{1,0:T(8,128)S(1)}, f32[8,128]{1,0:T(8,128)S(1)}, u32[]{:S(2)}, u32[]{:S(2)}) collective-permute-start(f32[8,128]{1,0:T(8,128)S(1)} %get-tuple-element.27.line_ref), channel_id=1, source_target_pairs={{0,16},{4,20},{8,24},{12,28},{16,0},{20,4},{24,8},{28,12},{1,17},{... | collective-permute-start | bytes 12296 | tf_op jit(solution)/shard_map/ppermute | solution.py:283
  32.5 3.0 %collective-permute-start.14 = (f32[8,128]{1,0:T(8,128)S(1)}, f32[8,128]{1,0:T(8,128)S(1)}, u32[]{:S(2)}, u32[]{:S(2)}) collective-permute-start(f32[8,128]{1,0:T(8,128)S(1)} %get-tuple-element.27.line_ref), channel_id=1, source_target_pairs={{0,20},{4,16},{8,28},{12,24},{16,4},{20,0},{24,12},{28,8},{1,21},{... | collective-permute-start | bytes 12296 | tf_op jit(solution)/shard_map/ppermute | solution.py:283

commit v4 on v3

--- a/solution.py
+++ b/solution.py
@@ -97,9 +97,9 @@
         full = expand(block_ref, pl.multiple_of(c * span, 128), *sizes)
         rate = 1.0 / full[dims + SCALE : dims + SCALE + 1]
         depth = 3 * full.shape[0]
-        turned = jnp.concatenate([full] * 3 + [jnp.broadcast_to(rate, (128 - depth, local))], axis=0).T
-        right = turned[:, :depth].astype(BF16)
-        rate = jnp.concatenate([jnp.broadcast_to(turned[:, depth : depth + 1], (local, 128))] * (tall // 128), axis=1)
+        rows16 = full.astype(BF16)
+        right = jnp.concatenate([rows16] * 3 + [jnp.zeros((128 - depth, local), BF16)], axis=0).T[:, :depth]
+        rate = jnp.concatenate([jnp.broadcast_to(rate, (128, local)).T] * (tall // 128), axis=1)
         block = full[dims:].astype(BF16)
         for m in range(top, rows, tall):
             exponent = jnp.dot(right, left_ref[:, m : m + tall], preferred_element_type=F32)

time: 36.5 us -> 36.5 us (level)
  no operation moved by 1% of the time
where the time goes in v4:
time: 36.5 us; the launch traced here: 36.3 us
  starting transfers between devices  17.5 us (48%)
  waiting for transfers between devices  9.61 us (26%)
  Pallas kernels  9.2 us (25%)
    pallas_call x13, Pallas kernels, call(): pl.pallas_call(kernel, out_shape=jax.tree.map(lambda s: pltpu.VMEM(s.shap...  9.2 us
    ppermute x3, starting transfers between devices, along(): lax.ppermute(x, 'col', list(enumerate(partners(n_col, step))))  5.23 us
    ppermute x4, starting transfers between devices, odd_only(): return lax.ppermute(x, ('row', 'col'), pairs)  5.11 us
    ppermute x4, waiting for transfers between devices, odd_only(): return lax.ppermute(x, ('row', 'col'), pairs)  4.96 us
    ppermute x2, starting transfers between devices, across(): lax.ppermute(x, 'row', [(4 * i + k, 4 * j + k) for i, j in enumerate(part...  3.1 us
    ppermute x2, waiting for transfers between devices, odd_across(): lax.ppermute(x, 'row', [(i, place(i, step)) for i in range(n_row)])  2.17 us
    ppermute x2, starting transfers between devices, odd_across(): lax.ppermute(x, 'row', [(i, place(i, step)) for i in range(n_row)])  1.8 us
    ppermute x1, starting transfers between devices, to_buddy(): return lax.ppermute(x, 'row', [(i, i ^ 2) for i in range(n_row)])  1.56 us
  transfers between devices with their start and end apart: 15, of which 8 were waited for; matrix products, arithmetic and copies ran while one was open for 0% of the time, Pallas kernels for 13%

profile of v4, /device:TPU:0, one launch (start us, length us, event | category | flops | bytes accessed | tf_op | source)
XLA Modules:
  0.0 36.3 jit_solution(6145411707230581587)
XLA Ops:
  0.0 0.7 %shard_map.37.refs_0_.own_ref = bf16[8,1664]{1,0:T(8,128)(2,1)S(1)} custom-call(bf16[16,512]{1,0:T(8,128)(2,1)} %points_ref.1, bf16[512]{0:T(512)(128)(2,1)} %spread_ref.1, bf16[8,512]{1,0:T(8,128)(2,1)} %vectors_ref.1), custom_call_target="tpu_custom_call" | custom-call | flops 1000000 | bytes 100000 | tf_op jit(solution)/shard_map/pallas_call | solution.py:20
  0.7 0.6 %collective-permute-start = (bf16[8,1664]{1,0:T(8,128)(2,1)S(1)}, bf16[8,1664]{1,0:T(8,128)(2,1)S(1)}, u32[]{:S(2)}, u32[]{:S(2)}) collective-permute-start(bf16[8,1664]{1,0:T(8,128)(2,1)S(1)} %shard_map.37.refs_0_.own_ref), channel_id=1, source_target_pairs={{0,4},{4,0},{8,12},{12,8},{16,20},{20,16},{24,28},{28,24},{1,5},{5... | collective-permute-start | bytes 79880 | tf_op jit(solution)/shard_map/ppermute | solution.py:254
  1.3 2.6 %collective-permute-start.2 = (bf16[8,1664]{1,0:T(8,128)(2,1)S(1)}, bf16[8,1664]{1,0:T(8,128)(2,1)S(1)}, u32[]{:S(2)}, u32[]{:S(2)}) collective-permute-start(bf16[8,1664]{1,0:T(8,128)(2,1)S(1)} %shard_map.37.refs_0_.own_ref), channel_id=1, source_target_pairs={{0,1},{1,0},{2,3},{3,2},{4,5},{5,4},{6,7},{7,6},{8,9},{9,8},{10,11... | collective-permute-start | bytes 79880 | tf_op jit(solution)/shard_map/ppermute | solution.py:257
  3.9 2.5 %collective-permute-start.3 = (bf16[8,1664]{1,0:T(8,128)(2,1)S(1)}, bf16[8,1664]{1,0:T(8,128)(2,1)S(1)}, u32[]{:S(2)}, u32[]{:S(2)}) collective-permute-start(bf16[8,1664]{1,0:T(8,128)(2,1)S(1)} %shard_map.37.refs_0_.own_ref), channel_id=1, source_target_pairs={{0,3},{1,2},{2,1},{3,0},{4,7},{5,6},{6,5},{7,4},{8,11},{9,10},{10,... | collective-permute-start | bytes 79880 | tf_op jit(solution)/shard_map/ppermute | solution.py:257
  6.4 0.1 collective-permute-start.4
  6.5 1.5 %collective-permute-start.5 = (bf16[8,1664]{1,0:T(8,128)(2,1)S(1)}, bf16[8,1664]{1,0:T(8,128)(2,1)S(1)}, u32[]{:S(2)}, u32[]{:S(2)}) collective-permute-start(bf16[8,1664]{1,0:T(8,128)(2,1)S(1)} %shard_map.37.refs_0_.own_ref), channel_id=1, source_target_pairs={{0,16},{4,20},{8,24},{12,28},{16,0},{20,4},{24,8},{28,12},{1,17},{... | collective-permute-start | bytes 79880 | tf_op jit(solution)/shard_map/ppermute | solution.py:264
  8.1 1.6 %collective-permute-start.1 = (bf16[8,3328]{1,0:T(8,128)(2,1)S(1)}, bf16[8,3328]{1,0:T(8,128)(2,1)S(1)}, u32[]{:S(2)}, u32[]{:S(2)}) collective-permute-start(bf16[8,3328]{1,0:T(8,128)(2,1)S(1)} %shard_map.38), channel_id=1, source_target_pairs={{0,8},{4,12},{8,0},{12,4},{16,24},{20,28},{24,16},{28,20},{1,9},{5... | collective-permute-start | bytes 159752 | tf_op jit(solution)/shard_map/ppermute | solution.py:260
  9.6 0.6 %shard_map.39 = (bf16[96,1024]{1,0:T(8,128)(2,1)S(1)}, f32[16,1024]{1,0:T(8,128)S(1)}) custom-call(bf16[8,1664]{1,0:T(8,128)(2,1)S(1)} %shard_map.37.refs_0_.own_ref, bf16[8,1664]{1,0:T(8,128)(2,1)S(1)} %collective-permute-done.refs_1_.mate_ref), custom_call_target="tpu_custom_call" | custom-call | flops 335544320 | bytes 1000000 | tf_op jit(solution)/shard_map/pallas_call | solution.py:20
  10.2 1.2 %collective-permute-done.4.refs_0_.early_ref = bf16[8,1664]{1,0:T(8,128)(2,1)S(1)} collective-permute-done((bf16[8,1664]{1,0:T(8,128)(2,1)S(1)}, bf16[8,1664]{1,0:T(8,128)(2,1)S(1)}, u32[]{:S(2)}, u32[]{:S(2)}) %collective-permute-start.4) | collective-permute-done | bytes 26656 | tf_op jit(solution)/shard_map/ppermute | solution.py:257
  11.5 0.6 %shard_map.40.part_ref = f32[16,1024]{1,0:T(8,128)S(1)} custom-call(bf16[96,1024]{1,0:T(8,128)(2,1)S(1)} %get-tuple-element.19.left_ref.upper_ref, f32[16,1024]{1,0:T(8,128)S(1)} %get-tuple-element.18.part_ref, bf16[8,1664]{1,0:T(8,128)(2,1)S(1)} %collective-permute-done.4.refs_0_.early_ref), custom_call_target="tpu_custom_call" | custom-call | flops 335544320 | bytes 1000000 | tf_op jit(solution)/shard_map/pallas_call | solution.py:20
  12.1 1.6 %collective-permute-start.6 = (bf16[8,4992]{1,0:T(8,128)(2,1)S(1)}, bf16[8,4992]{1,0:T(8,128)(2,1)S(1)}, u32[]{:S(2)}, u32[]{:S(2)}) collective-permute-start(bf16[8,4992]{1,0:T(8,128)(2,1)S(1)} %shard_map.44), channel_id=1, source_target_pairs={{0,16},{4,20},{8,24},{12,28},{16,0},{20,4},{24,8},{28,12},{1,17},{... | collective-permute-start | bytes 239624 | tf_op jit(solution)/shard_map/ppermute | solution.py:264
  13.7 0.1 shard_map.41
  13.8 2.3 %shard_map.42.part_ref = f32[16,2048]{1,0:T(8,128)S(1)} custom-call(bf16[96,2048]{1,0:T(8,128)(2,1)S(1)} %get-tuple-element.21.left_ref, f32[16,2048]{1,0:T(8,128)S(1)} %get-tuple-element.22.part_ref, bf16[8,1664]{1,0:T(8,128)(2,1)S(1)} %collective-permute-done.4.refs_0_.early_ref, bf16[8,1664]{1,0:T(8,128)(2,1)S(1)} %collective-permute-done.2.refs_0_.refs_1_, ...), custom_call_target="tpu_custom_call" | custom-call | flops 2013265920 | bytes 1000000 | tf_op jit(solution)/shard_map/pallas_call | solution.py:20
  16.1 1.0 %shard_map.43.part_ref = f32[16,2048]{1,0:T(8,128)S(1)} custom-call(bf16[96,2048]{1,0:T(8,128)(2,1)S(1)} %get-tuple-element.21.left_ref, f32[16,2048]{1,0:T(8,128)S(1)} %shard_map.42.part_ref, bf16[8,1664]{1,0:T(8,128)(2,1)S(1)} %collective-permute-done.5.refs_0_), custom_call_target="tpu_custom_call" | custom-call | flops 671088640 | bytes 1000000 | tf_op jit(solution)/shard_map/pallas_call | solution.py:20
  17.2 2.7 %shard_map.45.mine_ref = f32[8,2304]{1,0:T(8,128)S(1)} custom-call(bf16[96,2048]{1,0:T(8,128)(2,1)S(1)} %get-tuple-element.21.left_ref, f32[16,2048]{1,0:T(8,128)S(1)} %shard_map.43.part_ref, bf16[8,4992]{1,0:T(8,128)(2,1)S(1)} %collective-permute-done.6.refs_0_), custom_call_target="tpu_custom_call" | custom-call | flops 2013265920 | bytes 1000000 | tf_op jit(solution)/shard_map/pallas_call | solution.py:20
  19.9 0.0 collective-permute-start.7
  20.0 1.3 %collective-permute-done.7.other_ref = f32[8,2304]{1,0:T(8,128)S(1)} collective-permute-done((f32[8,2304]{1,0:T(8,128)S(1)}, f32[8,2304]{1,0:T(8,128)S(1)}, u32[]{:S(2)}, u32[]{:S(2)}) %collective-permute-start.7) | collective-permute-done | bytes 73760 | tf_op jit(solution)/shard_map/ppermute | solution.py:254
  21.3 1.6 %collective-permute-start.8 = (f32[8,2304]{1,0:T(8,128)S(1)}, f32[8,2304]{1,0:T(8,128)S(1)}, u32[]{:S(2)}, u32[]{:S(2)}) collective-permute-start(f32[8,2304]{1,0:T(8,128)S(1)} %shard_map.46.mine_ref), channel_id=1, source_target_pairs={{0,8},{1,9},{2,10},{3,11},{4,12},{5,13},{6,14},{7,15},{8,0},{9,1},... | collective-permute-start | bytes 221192 | tf_op jit(solution)/shard_map/ppermute | solution.py:275
  22.8 2.9 %collective-permute-done.8.other_ref = f32[8,2304]{1,0:T(8,128)S(1)} collective-permute-done((f32[8,2304]{1,0:T(8,128)S(1)}, f32[8,2304]{1,0:T(8,128)S(1)}, u32[]{:S(2)}, u32[]{:S(2)}) %collective-permute-start.8) | collective-permute-done | bytes 73760 | tf_op jit(solution)/shard_map/ppermute | solution.py:275
  25.7 0.1 shard_map.47
  25.8 1.5 %collective-permute-start.9 = (f32[8,128]{1,0:T(8,128)S(1)}, f32[8,128]{1,0:T(8,128)S(1)}, u32[]{:S(2)}, u32[]{:S(2)}) collective-permute-start(f32[8,128]{1,0:T(8,128)S(1)} %get-tuple-element.26.refs_0_), channel_id=1, source_target_pairs={{0,8},{1,9},{2,10},{3,11},{4,5},{5,4},{6,7},{7,6},{8,0},{9,1},{10,... | collective-permute-start | bytes 12296 | tf_op jit(solution)/shard_map/ppermute | solution.py:275
  27.3 0.5 %collective-permute-start.10 = (f32[8,128]{1,0:T(8,128)S(1)}, f32[8,128]{1,0:T(8,128)S(1)}, u32[]{:S(2)}, u32[]{:S(2)}) collective-permute-start(f32[8,128]{1,0:T(8,128)S(1)} %get-tuple-element.26.refs_0_), channel_id=1, source_target_pairs={{0,8},{1,9},{2,10},{3,11},{4,6},{5,7},{6,4},{7,5},{8,0},{9,1},{10,... | collective-permute-start | bytes 12296 | tf_op jit(solution)/shard_map/ppermute | solution.py:275
  27.9 1.5 %collective-permute-start.11 = (f32[8,128]{1,0:T(8,128)S(1)}, f32[8,128]{1,0:T(8,128)S(1)}, u32[]{:S(2)}, u32[]{:S(2)}) collective-permute-start(f32[8,128]{1,0:T(8,128)S(1)} %get-tuple-element.26.refs_0_), channel_id=1, source_target_pairs={{0,8},{1,9},{2,10},{3,11},{4,7},{5,6},{6,5},{7,4},{8,0},{9,1},{10,... | collective-permute-start | bytes 12296 | tf_op jit(solution)/shard_map/ppermute | solution.py:275
  29.4 0.1 collective-permute-done.9.refs_1_
  29.5 1.5 %collective-permute-done.10.refs_2_ = f32[8,128]{1,0:T(8,128)S(1)} collective-permute-done((f32[8,128]{1,0:T(8,128)S(1)}, f32[8,128]{1,0:T(8,128)S(1)}, u32[]{:S(2)}, u32[]{:S(2)}) %collective-permute-start.10) | collective-permute-done | bytes 4128 | tf_op jit(solution)/shard_map/ppermute | solution.py:275
  31.0 0.5 %collective-permute-done.11.refs_3_ = f32[8,128]{1,0:T(8,128)S(1)} collective-permute-done((f32[8,128]{1,0:T(8,128)S(1)}, f32[8,128]{1,0:T(8,128)S(1)}, u32[]{:S(2)}, u32[]{:S(2)}) %collective-permute-start.11) | collective-permute-done | bytes 4128 | tf_op jit(solution)/shard_map/ppermute | solution.py:275
  31.5 0.1 collective-permute-start.12
  31.6 0.9 %collective-permute-start.13 = (f32[8,128]{1,0:T(8,128)S(1)}, f32[8,128]{1,0:T(8,128)S(1)}, u32[]{:S(2)}, u32[]{:S(2)}) collective-permute-start(f32[8,128]{1,0:T(8,128)S(1)} %get-tuple-element.27.line_ref), channel_id=1, source_target_pairs={{0,16},{4,20},{8,24},{12,28},{16,0},{20,4},{24,8},{28,12},{1,17},{... | collective-permute-start | bytes 12296 | tf_op jit(solution)/shard_map/ppermute | solution.py:283
  32.5 0.9 %collective-permute-start.14 = (f32[8,128]{1,0:T(8,128)S(1)}, f32[8,128]{1,0:T(8,128)S(1)}, u32[]{:S(2)}, u32[]{:S(2)}) collective-permute-start(f32[8,128]{1,0:T(8,128)S(1)} %get-tuple-element.27.line_ref), channel_id=1, source_target_pairs={{0,20},{4,16},{8,28},{12,24},{16,4},{20,0},{24,12},{28,8},{1,21},{... | collective-permute-start | bytes 12296 | tf_op jit(solution)/shard_map/ppermute | solution.py:283
  33.4 1.8 %collective-permute-done.13.refs_0_ = f32[8,128]{1,0:T(8,128)S(1)} collective-permute-done((f32[8,128]{1,0:T(8,128)S(1)}, f32[8,128]{1,0:T(8,128)S(1)}, u32[]{:S(2)}, u32[]{:S(2)}) %collective-permute-start.13) | collective-permute-done | bytes 4128 | tf_op jit(solution)/shard_map/ppermute | solution.py:283
  35.2 0.4 collective-permute-done.14.refs_1_
  35.5 0.8 %shard_map.49 = f32[8,512]{1,0:T(8,128)} custom-call(f32[8,1024]{1,0:T(8,128)S(1)} %get-tuple-element.25.update_ref, f32[8,128]{1,0:T(8,128)S(1)} %get-tuple-element.27.line_ref, f32[8,640]{1,0:T(8,128)S(1)} %collective-permute-done.12.given_ref, f32[8,128]{1,0:T(8,128)S(1)} %collective-permute-done.13.refs_0_, f32[8,128]{1,0:T(8,128)S(1)} %collective-permute-done.14.refs_1_), custom_call_target="tpu_custom_call" | custom-call | flops 1000000 | bytes 100000 | tf_op jit(solution)/shard_map/pallas_call | solution.py:20
  (11 shorter events, 0.1 us)
Async XLA Ops:
  0.7 7.3 %collective-permute-start = (bf16[8,1664]{1,0:T(8,128)(2,1)S(1)}, bf16[8,1664]{1,0:T(8,128)(2,1)S(1)}, u32[]{:S(2)}, u32[]{:S(2)}) collective-permute-start(bf16[8,1664]{1,0:T(8,128)(2,1)S(1)} %shard_map.37.refs_0_.own_ref), channel_id=1, source_target_pairs={{0,4},{4,0},{8,12},{12,8},{16,20},{20,16},{24,28},{28,24},{1,5},{5... | collective-permute-start | bytes 79880 | tf_op jit(solution)/shard_map/ppermute | solution.py:254
  1.3 10.8 %collective-permute-start.2 = (bf16[8,1664]{1,0:T(8,128)(2,1)S(1)}, bf16[8,1664]{1,0:T(8,128)(2,1)S(1)}, u32[]{:S(2)}, u32[]{:S(2)}) collective-permute-start(bf16[8,1664]{1,0:T(8,128)(2,1)S(1)} %shard_map.37.refs_0_.own_ref), channel_id=1, source_target_pairs={{0,1},{1,0},{2,3},{3,2},{4,5},{5,4},{6,7},{7,6},{8,9},{9,8},{10,11... | collective-permute-start | bytes 79880 | tf_op jit(solution)/shard_map/ppermute | solution.py:257
  3.9 8.1 %collective-permute-start.3 = (bf16[8,1664]{1,0:T(8,128)(2,1)S(1)}, bf16[8,1664]{1,0:T(8,128)(2,1)S(1)}, u32[]{:S(2)}, u32[]{:S(2)}) collective-permute-start(bf16[8,1664]{1,0:T(8,128)(2,1)S(1)} %shard_map.37.refs_0_.own_ref), channel_id=1, source_target_pairs={{0,3},{1,2},{2,1},{3,0},{4,7},{5,6},{6,5},{7,4},{8,11},{9,10},{10,... | collective-permute-start | bytes 79880 | tf_op jit(solution)/shard_map/ppermute | solution.py:257
  6.4 5.0 %collective-permute-start.4 = (bf16[8,1664]{1,0:T(8,128)(2,1)S(1)}, bf16[8,1664]{1,0:T(8,128)(2,1)S(1)}, u32[]{:S(2)}, u32[]{:S(2)}) collective-permute-start(bf16[8,1664]{1,0:T(8,128)(2,1)S(1)} %shard_map.37.refs_0_.own_ref), channel_id=1, source_target_pairs={{0,2},{1,3},{2,0},{3,1},{4,6},{5,7},{6,4},{7,5},{8,10},{9,11},{10,... | collective-permute-start | bytes 79880 | tf_op jit(solution)/shard_map/ppermute | solution.py:257
  6.5 9.6 %collective-permute-start.5 = (bf16[8,1664]{1,0:T(8,128)(2,1)S(1)}, bf16[8,1664]{1,0:T(8,128)(2,1)S(1)}, u32[]{:S(2)}, u32[]{:S(2)}) collective-permute-start(bf16[8,1664]{1,0:T(8,128)(2,1)S(1)} %shard_map.37.refs_0_.own_ref), channel_id=1, source_target_pairs={{0,16},{4,20},{8,24},{12,28},{16,0},{20,4},{24,8},{28,12},{1,17},{... | collective-permute-start | bytes 79880 | tf_op jit(solution)/shard_map/ppermute | solution.py:264
  8.1 5.6 %collective-permute-start.1 = (bf16[8,3328]{1,0:T(8,128)(2,1)S(1)}, bf16[8,3328]{1,0:T(8,128)(2,1)S(1)}, u32[]{:S(2)}, u32[]{:S(2)}) collective-permute-start(bf16[8,3328]{1,0:T(8,128)(2,1)S(1)} %shard_map.38), channel_id=1, source_target_pairs={{0,8},{4,12},{8,0},{12,4},{16,24},{20,28},{24,16},{28,20},{1,9},{5... | collective-permute-start | bytes 159752 | tf_op jit(solution)/shard_map/ppermute | solution.py:260
  12.1 5.1 %collective-permute-start.6 = (bf16[8,4992]{1,0:T(8,128)(2,1)S(1)}, bf16[8,4992]{1,0:T(8,128)(2,1)S(1)}, u32[]{:S(2)}, u32[]{:S(2)}) collective-permute-start(bf16[8,4992]{1,0:T(8,128)(2,1)S(1)} %shard_map.44), channel_id=1, source_target_pairs={{0,16},{4,20},{8,24},{12,28},{16,0},{20,4},{24,8},{28,12},{1,17},{... | collective-permute-start | bytes 239624 | tf_op jit(solution)/shard_map/ppermute | solution.py:264
  19.9 1.3 %collective-permute-start.7 = (f32[8,2304]{1,0:T(8,128)S(1)}, f32[8,2304]{1,0:T(8,128)S(1)}, u32[]{:S(2)}, u32[]{:S(2)}) collective-permute-start(f32[8,2304]{1,0:T(8,128)S(1)} %shard_map.45.mine_ref), channel_id=1, source_target_pairs={{0,4},{4,0},{8,12},{12,8},{16,20},{20,16},{24,28},{28,24},{1,5},{5... | collective-permute-start | bytes 221192 | tf_op jit(solution)/shard_map/ppermute | solution.py:254
  21.3 4.4 %collective-permute-start.8 = (f32[8,2304]{1,0:T(8,128)S(1)}, f32[8,2304]{1,0:T(8,128)S(1)}, u32[]{:S(2)}, u32[]{:S(2)}) collective-permute-start(f32[8,2304]{1,0:T(8,128)S(1)} %shard_map.46.mine_ref), channel_id=1, source_target_pairs={{0,8},{1,9},{2,10},{3,11},{4,12},{5,13},{6,14},{7,15},{8,0},{9,1},... | collective-permute-start | bytes 221192 | tf_op jit(solution)/shard_map/ppermute | solution.py:275
  25.8 3.6 %collective-permute-start.9 = (f32[8,128]{1,0:T(8,128)S(1)}, f32[8,128]{1,0:T(8,128)S(1)}, u32[]{:S(2)}, u32[]{:S(2)}) collective-permute-start(f32[8,128]{1,0:T(8,128)S(1)} %get-tuple-element.26.refs_0_), channel_id=1, source_target_pairs={{0,8},{1,9},{2,10},{3,11},{4,5},{5,4},{6,7},{7,6},{8,0},{9,1},{10,... | collective-permute-start | bytes 12296 | tf_op jit(solution)/shard_map/ppermute | solution.py:275
  27.3 3.6 %collective-permute-start.10 = (f32[8,128]{1,0:T(8,128)S(1)}, f32[8,128]{1,0:T(8,128)S(1)}, u32[]{:S(2)}, u32[]{:S(2)}) collective-permute-start(f32[8,128]{1,0:T(8,128)S(1)} %get-tuple-element.26.refs_0_), channel_id=1, source_target_pairs={{0,8},{1,9},{2,10},{3,11},{4,6},{5,7},{6,4},{7,5},{8,0},{9,1},{10,... | collective-permute-start | bytes 12296 | tf_op jit(solution)/shard_map/ppermute | solution.py:275
  27.9 3.6 %collective-permute-start.11 = (f32[8,128]{1,0:T(8,128)S(1)}, f32[8,128]{1,0:T(8,128)S(1)}, u32[]{:S(2)}, u32[]{:S(2)}) collective-permute-start(f32[8,128]{1,0:T(8,128)S(1)} %get-tuple-element.26.refs_0_), channel_id=1, source_target_pairs={{0,8},{1,9},{2,10},{3,11},{4,7},{5,6},{6,5},{7,4},{8,0},{9,1},{10,... | collective-permute-start | bytes 12296 | tf_op jit(solution)/shard_map/ppermute | solution.py:275
  31.5 4.0 %collective-permute-start.12 = (f32[8,640]{1,0:T(8,128)S(1)}, f32[8,640]{1,0:T(8,128)S(1)}, u32[]{:S(2)}, u32[]{:S(2)}) collective-permute-start(f32[8,640]{1,0:T(8,128)S(1)} %get-tuple-element.28), channel_id=1, source_target_pairs={{0,4},{4,0},{8,12},{12,8},{16,20},{20,16},{24,28},{28,24},{1,5},{5... | collective-permute-start | bytes 61448 | tf_op jit(solution)/shard_map/ppermute | solution.py:254
  31.6 3.6 %collective-permute-start.13 = (f32[8,128]{1,0:T(8,128)S(1)}, f32[8,128]{1,0:T(8,128)S(1)}, u32[]{:S(2)}, u32[]{:S(2)}) collective-permute-start(f32[8,128]{1,0:T(8,128)S(1)} %get-tuple-element.27.line_ref), channel_id=1, source_target_pairs={{0,16},{4,20},{8,24},{12,28},{16,0},{20,4},{24,8},{28,12},{1,17},{... | collective-permute-start | bytes 12296 | tf_op jit(solution)/shard_map/ppermute | solution.py:283
  32.5 3.0 %collective-permute-start.14 = (f32[8,128]{1,0:T(8,128)S(1)}, f32[8,128]{1,0:T(8,128)S(1)}, u32[]{:S(2)}, u32[]{:S(2)}) collective-permute-start(f32[8,128]{1,0:T(8,128)S(1)} %get-tuple-element.27.line_ref), channel_id=1, source_target_pairs={{0,20},{4,16},{8,28},{12,24},{16,4},{20,0},{24,12},{28,8},{1,21},{... | collective-permute-start | bytes 12296 | tf_op jit(solution)/shard_map/ppermute | solution.py:283
